TPU v7x, 512 devices: a whole 4x4x16 slice. The times are simulated.
512 devices in a mesh: dp: 64 (over y, z), tensor: 8 (over x, core).
Axes of the slice: x: 4, y: 4, z: 16, core: 2. Of those that a mesh axis runs over, the one named last changes fastest.
Arguments:
- grad_kv: bfloat16 [64, 2, 512, 2048], P('dp', None, 'tensor'), may hold values from -16 to 16
- error_kv: bfloat16 [64, 2, 512, 2048], P('dp', None, 'tensor'), may hold values from -4 to 4
- moment_kv: bfloat16 [64, 2, 512, 2048], P('dp', None, 'tensor'), may hold values from -6 to 6
- start_dirs: float32 [2, 32, 2048], replicated, may hold values from -6 to 6
- weight_kv: float32 [2, 512, 2048], P(None, 'tensor', 'dp'), may hold values from -6 to 6
- norm_grads: bfloat16 [64, 2, 2048], P('dp', None, 'tensor'), may hold values from -16 to 16
- norm_gains: float32 [2, 8, 256], P(None, 'tensor', 'dp'), may hold values from 0.5 to 1.5
Outputs:
- new_weight_kv: float32 [2, 512, 2048], P(None, 'tensor', 'dp')
- new_error_kv: bfloat16 [64, 2, 512, 2048], P('dp', None, 'tensor')
- new_moment_kv: bfloat16 [64, 2, 512, 2048], P('dp', None, 'tensor')
- new_gains: float32 [2, 8, 256], P(None, 'tensor', 'dp')
All inputs are finite; a program needn't handle non-finite values.
Results may differ from a plain program's by a relative error of at most 0.001.
Values sent between devices are 32-bit elements; how exact they have to be, the bound alone decides.
No kernel may reach another device: no remote copies, remote signals or barrier semaphores. Data moves between devices by JAX's collectives and lax.ppermute only.
A program may use at most 64 MiB of HBM per device.

v0:
```python
import jax
import jax.numpy as jnp
from jax import lax
from jax.sharding import PartitionSpec as P

momentum_decay = 0.9
step_size = 0.5


def project(inputs, directions):
    return jnp.einsum("mrd,mkd->mrk", inputs, directions, precision=lax.Precision.HIGHEST)


def tri_solve(triangle, columns):
    return jax.scipy.linalg.solve_triangular(triangle, columns, lower=True)


def orthonormal(factor):
    full_rows = lax.all_gather(factor, "tensor", axis=1, tiled=True)
    gram_matrix = jnp.einsum("mrk,mrj->mkj", full_rows, full_rows, precision=lax.Precision.HIGHEST)
    cholesky_factor = jnp.linalg.cholesky(gram_matrix)
    solved = jax.vmap(tri_solve)(cholesky_factor, jnp.swapaxes(factor, 1, 2))
    return jnp.swapaxes(solved, 1, 2)


def column_sums(inputs, basis):
    partial_sum = jnp.einsum("mrd,mrk->mkd", inputs, basis, precision=lax.Precision.HIGHEST)
    summed = lax.psum(partial_sum, ("dp", "tensor"))
    return summed


def shards(grad_kv, error_kv, moment_kv, start_dirs, weight_kv, norm_grads, norm_gains):
    replicas = lax.axis_size("dp")
    dp_index = lax.axis_index("dp")
    moment_f = momentum_decay * moment_kv.astype(jnp.float32) + grad_kv.astype(jnp.float32)
    new_moment_kv = moment_f.astype(jnp.bfloat16)
    inputs = (moment_f + error_kv.astype(jnp.float32))[0]
    norm_terms = norm_grads[0].astype(jnp.float32)
    gain_cols = norm_gains.shape[2]
    factor = project(inputs, start_dirs)
    factor, norm_total = lax.psum((factor, norm_terms), "dp")
    own_norm = lax.dynamic_slice_in_dim(norm_total, dp_index * gain_cols, gain_cols, 1)
    mean_norm = own_norm / replicas
    basis = orthonormal(factor)
    directions = column_sums(inputs, basis)
    factor = lax.psum(project(inputs, directions), "dp")
    basis = orthonormal(factor)
    directions = column_sums(inputs, basis)
    approx = (
        jnp.einsum("mrk,mkd->mrd", basis, directions, precision=lax.Precision.HIGHEST) / replicas
    )
    new_error_kv = (inputs - approx).astype(jnp.bfloat16)[None]
    weight_cols = weight_kv.shape[2]
    own_approx = lax.dynamic_slice_in_dim(approx, dp_index * weight_cols, weight_cols, 2)
    new_weight_kv = weight_kv - step_size * own_approx
    new_gains = norm_gains - step_size * mean_norm[:, None, :]
    return (new_weight_kv, new_error_kv, new_moment_kv, new_gains)


def solution(mesh):
    return jax.shard_map(
        shards,
        mesh=mesh,
        in_specs=(
            P("dp", None, "tensor", None),
            P("dp", None, "tensor", None),
            P("dp", None, "tensor", None),
            P(),
            P(None, "tensor", "dp"),
            P("dp", None, "tensor"),
            P(None, "tensor", "dp"),
        ),
        out_specs=(
            P(None, "tensor", "dp"),
            P("dp", None, "tensor", None),
            P("dp", None, "tensor", None),
            P(None, "tensor", "dp"),
        ),
        check_vma=False,
    )
```

profile of v0, /device:TPU:1, one launch (start us, length us, event | category | flops | bytes accessed | tf_op | source)
XLA Modules:
  0.0 1548.8 jit_solution(6720480289268949113)
XLA Ops:
  7.3 1.0 copy-done
  8.2 2.6 fusion.6
  10.8 231.6 %psum.35 = f32[2,64,32]{1,2,0:T(8,128)S(1)} all-reduce(f32[2,64,32]{1,2,0:T(8,128)S(1)} %fusion.6), channel_id=1, replica_groups=mesh['dp'=64,'tensor'=8] {'dp'}, use_global_device_ids=true, to_apply=%region_0.0 | all-reduce | flops 4096 | bytes 32768 | tf_op jit(solution)/shard_map/psum | solution.py:41
  242.4 69.2 %all_gather.6 = f32[2,512,32]{2,0,1:T(2,128)S(1)} all-gather(f32[2,64,32]{2,0,1:T(2,128)S(1)} %copy.31), channel_id=1, replica_groups=mesh['dp'=64,'tensor'=8] {'tensor'}, dimensions={1}, use_global_device_ids=true | all-gather | bytes 147456 | tf_op jit(solution)/shard_map/all_gather | solution.py:19
  311.7 1.0 fusion.13
  312.8 5.9 custom-call.8
  318.9 4.9 custom-call.9
  324.1 1.6 fusion.4
  325.8 0.6 copy-done.5
  326.4 451.8 %all-reduce.4.cloned.1.call-done = f32[2,32,2048]{2,1,0:T(8,128)} async-done(((f32[2,32,2048]{2,1,0:T(8,128)}), f32[2,32,2048]{2,1,0:T(8,128)}) %all-reduce.4.cloned.1.call-update) | async-done | bytes 524304 | tf_op jit(solution)/shard_map/psum | solution.py:28
  778.2 2.2 fusion.2
  780.5 223.7 %all-reduce = (f32[2,64,32]{1,2,0:T(8,128)S(1)}, f32[2,256]{1,0:T(2,128)S(1)}) all-reduce(f32[2,64,32]{1,2,0:T(8,128)S(1)} %fusion.2, f32[2,256]{1,0:T(2,128)S(1)} %bitcast_convert_fusion), channel_id=1, replica_groups=mesh['dp'=64,'tensor'=8] {'dp'}, use_global_device_ids=true, to_apply=%region_4.0 | all-reduce | flops 4608 | bytes 36864 | tf_op jit(solution)/shard_map/psum | solution.py:46
  1004.2 67.9 %all_gather.7 = f32[2,512,32]{2,0,1:T(2,128)S(1)} all-gather(f32[2,64,32]{2,0,1:T(2,128)S(1)} %copy.36), channel_id=1, replica_groups=mesh['dp'=64,'tensor'=8] {'tensor'}, dimensions={1}, use_global_device_ids=true | all-gather | bytes 147456 | tf_op jit(solution)/shard_map/all_gather | solution.py:19
  1072.1 1.0 fusion.11
  1073.2 5.9 custom-call.10
  1079.3 4.9 custom-call.11
  1084.5 1.6 fusion
  1086.2 1.0 fusion.9
  1087.3 0.7 copy-done.6
  1087.9 0.6 bitcast_subtract_fusion.1
  1088.6 449.4 %all-reduce.6.cloned.1.call-done = f32[2,32,2048]{2,1,0:T(8,128)} async-done(((f32[2,32,2048]{2,1,0:T(8,128)}), f32[2,32,2048]{2,1,0:T(8,128)}) %all-reduce.6.cloned.1.call-update) | async-done | bytes 524304 | tf_op jit(solution)/shard_map/psum | solution.py:28
  1538.0 2.1 convolution_multiply_fusion
  1540.1 1.1 fusion.10
  1541.3 0.7 copy.43
  (34 shorter events, 1.7 us)
Async XLA Ops:
  7.2 1.0 copy-start
  7.2 771.0 %all-reduce.4.cloned.1.call-start = ((), (), s32[]{:S(2)}) async-start(), calls=%async_computation | async-start | bytes 1048576 | tf_op jit(solution)/shard_map/psum | solution.py:28
  242.3 81.7 %copy-start.3 = (bf16[1,2,64,2048]{3,2,1,0:T(8,128)(2,1)S(1)}, bf16[1,2,64,2048]{3,2,1,0:T(8,128)(2,1)}, u32[]{:S(2)}) copy-start(bf16[1,2,64,2048]{3,2,1,0:T(8,128)(2,1)} %param.11) | copy-start | bytes 1572868
  242.4 81.7 %copy-start.2 = (bf16[1,2,64,2048]{3,2,1,0:T(8,128)(2,1)S(1)}, bf16[1,2,64,2048]{3,2,1,0:T(8,128)(2,1)}, u32[]{:S(2)}) copy-start(bf16[1,2,64,2048]{3,2,1,0:T(8,128)(2,1)} %param.12) | copy-start | bytes 1572868
  311.7 12.4 copy-start.1
  325.7 0.7 copy-start.5
  325.8 1212.2 %all-reduce.6.cloned.1.call-start = ((), (), s32[]{:S(2)}) async-start(), calls=%async_computation.1 | async-start | bytes 1048576 | tf_op jit(solution)/shard_map/psum | solution.py:28
  1086.2 1.0 copy-start.4
  1087.2 0.7 copy-start.6
Sparse Core Ops, SparseCore 0:
  325.9 452.2 all-reduce.3
  1086.3 451.6 all-reduce.5
where the time goes:
time: 1550 us
  waiting for transfers between devices  901 us (58%)
  blocking collectives  592 us (38%)
  other arithmetic  24.9 us (2%)
    psum x2, waiting for transfers between devices, column_sums(): summed = lax.psum(partial_sum, ('dp', 'tensor'))  901 us
    psum x1, blocking collectives, shards(): factor, norm_total = lax.psum((factor, norm_terms), 'dp')  232 us
    psum x1, blocking collectives, shards(): factor = lax.psum(project(inputs, directions), 'dp')  224 us
    all_gather x2, blocking collectives, orthonormal(): full_rows = lax.all_gather(factor, 'tensor', axis=1, tiled=True)  137 us
  transfers between devices with their start and end apart: 2, of which 2 were waited for; matrix products, arithmetic and copies ran while one was open for 0% of the time, Pallas kernels for 0%

commit v1 on v0

v1 whole, which is shorter than its diff:
```python
import jax
import jax.numpy as jnp
from jax import lax
from jax.sharding import Mesh
from jax.sharding import PartitionSpec as P

momentum_decay = 0.9
step_size = 0.5
Y_CHIPS = 4
CORES = 2
HIGH = lax.Precision.HIGHEST


def spread(value, axes, count):
    copies = jnp.broadcast_to(value[None], (count,) + value.shape)
    return lax.all_to_all(copies, axes, 0, 0, tiled=True)


def tri_solve(triangle, columns):
    return jax.scipy.linalg.solve_triangular(triangle, columns, lower=True)


def pack(product, gram):
    parts = (product[0], product[1], gram[0], gram[1])
    joined = jnp.concatenate(parts, axis=1)
    return jnp.pad(joined, ((0, 0), (0, -joined.shape[1] % 128)))


def shards(grad_kv, error_kv, moment_kv, start_dirs, weight_kv, norm_grads, norm_gains):
    n_y, n_z, n_x, n_core = (lax.axis_size(a) for a in ("y", "z", "x", "core"))
    replicas = n_y * n_z
    y, z, core = (lax.axis_index(a) for a in ("y", "z", "core"))
    _, n_mat, rows, width = grad_kv.shape
    rank = start_dirs.shape[1]
    groups = n_y * n_core
    cols = width // groups
    chip_rows = rows * n_core
    z_rows = chip_rows // n_z
    features = norm_grads.shape[2] // n_y
    gain_cols = norm_gains.shape[2]

    moment_f = momentum_decay * moment_kv.astype(jnp.float32) + grad_kv.astype(jnp.float32)
    new_moment_kv = moment_f.astype(jnp.bfloat16)
    inputs = (moment_f + error_kv.astype(jnp.float32))[0]

    own_factor = jnp.einsum("mrd,mkd->rmk", inputs, start_dirs, precision=HIGH).reshape(rows, n_mat * rank)
    blocks = inputs.reshape(n_mat, rows, groups, cols).transpose(2, 1, 0, 3).reshape(groups, rows, n_mat * cols)
    norm_terms = norm_grads[0].astype(jnp.float32).reshape(n_mat, n_y, features).transpose(1, 0, 2)
    norm_terms = jnp.pad(norm_terms, ((0, 0), (0, rows - n_mat), (0, 0)))
    norm_terms = jnp.repeat(norm_terms, n_core, axis=0)
    sent = jnp.concatenate(
        [blocks, jnp.broadcast_to(own_factor[None], (groups, rows, n_mat * rank)), norm_terms], axis=2
    )
    lanes = sent.shape[2]
    at_factor, at_norm = n_mat * cols, n_mat * (cols + rank)
    got = lax.all_to_all(sent, ("y", "core"), 0, 0, tiled=True)
    over_y = jnp.sum(got.reshape(n_y, n_core, rows, lanes), axis=0)
    norm_y = lax.dynamic_index_in_dim(over_y, core, 0, keepdims=False)[:z_rows, at_norm:]
    norm_y = jnp.broadcast_to(norm_y[None], (n_z, z_rows, features))
    over_y = over_y.reshape(n_z, z_rows, lanes)
    sent = jnp.concatenate([over_y[:, :, :at_norm], norm_y], axis=2)
    got = lax.all_to_all(sent, "z", 0, 0, tiled=True)
    over_z = jnp.sum(got, axis=0)
    own_norm = lax.dynamic_slice(over_z, (0, at_norm + z * gain_cols), (n_mat, gain_cols))
    mean_norm = own_norm / replicas
    total = lax.all_gather(over_z, "z", axis=0, tiled=True)
    matrix = total[:, :at_factor].reshape(chip_rows, n_mat, cols).transpose(1, 0, 2)
    factor = total[:, at_factor:at_norm].reshape(chip_rows, n_mat, rank).transpose(1, 0, 2)

    def right_factor(factor):
        product = jnp.einsum("mrk,mrc->mkc", factor, matrix, precision=HIGH)
        gram = jnp.einsum("mrk,mrj->mkj", factor, factor, precision=HIGH)
        summed = jnp.sum(lax.all_gather(pack(product, gram), "x"), axis=0)
        product = jnp.stack([summed[:, m * cols : (m + 1) * cols] for m in range(n_mat)])
        start = n_mat * cols
        gram = jnp.stack([summed[:, start + m * rank : start + (m + 1) * rank] for m in range(n_mat)])
        triangle = jnp.linalg.cholesky(gram)
        return triangle, jax.vmap(tri_solve)(triangle, product)

    _, directions = right_factor(factor)
    factor = jnp.einsum("mrc,mkc->rmk", matrix, directions, precision=HIGH).reshape(n_core, rows, n_mat * rank)
    factor = factor.transpose(1, 0, 2).reshape(rows, n_core * n_mat * rank)
    factor = jnp.sum(spread(factor, ("y", "core"), groups), axis=0)
    factor = factor.reshape(rows, n_core, n_mat, rank).transpose(2, 1, 0, 3)
    triangle, directions = right_factor(factor.reshape(n_mat, chip_rows, rank))
    own_rows = lax.dynamic_index_in_dim(factor, core, 1, keepdims=False)
    basis_t = jax.vmap(tri_solve)(triangle, jnp.swapaxes(own_rows, 1, 2))
    directions = spread(directions, ("y", "core"), groups)
    directions = directions.transpose(1, 2, 0, 3).reshape(n_mat, rank, width)
    approx = jnp.einsum("mkr,mkd->mrd", basis_t, directions, precision=HIGH) / replicas
    new_error_kv = (inputs - approx).astype(jnp.bfloat16)[None]
    weight_cols = weight_kv.shape[2]
    own_dirs = lax.dynamic_slice_in_dim(directions, (y * n_z + z) * weight_cols, weight_cols, 2)
    own_approx = jnp.einsum("mkr,mkd->mrd", basis_t, own_dirs, precision=HIGH) / replicas
    new_weight_kv = weight_kv - step_size * own_approx
    new_gains = norm_gains - step_size * mean_norm[:, None, :]
    return (new_weight_kv, new_error_kv, new_moment_kv, new_gains)


def solution(mesh):
    dp, tensor = mesh.devices.shape
    sizes = (Y_CHIPS, dp // Y_CHIPS, tensor // CORES, CORES)
    chips = Mesh(mesh.devices.reshape(sizes), ("y", "z", "x", "core"))
    dp, tensor = ("y", "z"), ("x", "core")
    return jax.shard_map(
        shards,
        mesh=chips,
        in_specs=(
            P(dp, None, tensor, None),
            P(dp, None, tensor, None),
            P(dp, None, tensor, None),
            P(),
            P(None, tensor, dp),
            P(dp, None, tensor),
            P(None, tensor, dp),
        ),
        out_specs=(
            P(None, tensor, dp),
            P(dp, None, tensor, None),
            P(dp, None, tensor, None),
            P(None, tensor, dp),
        ),
        check_vma=False,
    )
```

time: 1550 us -> 187 us (0.12)
  waiting for transfers between devices: 901 us -> 41 us
  blocking collectives: 592 us -> 70.9 us
  starting transfers between devices: 0.08 us -> 27.1 us
    psum x2 -> x0, waiting for transfers between devices: 901 us -> none  [column_sums(): summed = lax.psum(partial_sum, ('dp', 'tensor'))]
    psum x2 -> x0, blocking collectives: 455 us -> none  [the longest x1 232 us: shards(): factor, norm_total = lax.psum((factor, norm_terms), 'dp')]
    all_gather x2 -> x3, blocking collectives: 137 us -> 48.7 us  [the longest x1 28.3 us: shards(): total = lax.all_gather(over_z, 'z', axis=0, tiled=True)]
    all_to_all x0 -> x3, waiting for transfers between devices: none -> 41 us  [the longest x1 17.8 us: shards(): got = lax.all_to_all(sent, ('y', 'core'), 0, 0, tiled=True)]
    all_to_all x0 -> x3, starting transfers between devices: none -> 27.1 us  [the longest x1 10.5 us: shards(): got = lax.all_to_all(sent, 'z', 0, 0, tiled=True)]
    all_to_all x0 -> x1, blocking collectives: none -> 22.2 us  [spread(): return lax.all_to_all(copies, axes, 0, 0, tiled=True)]
  transfers between devices with their start and end apart: 2 -> 3, of which waited for: 2 -> 3; matrix products, arithmetic and copies ran while one was open for 0% -> 0% of each run, Pallas kernels for 0% -> 0%
where the time goes in v1:
time: 187 us; the launch traced here: 186 us
  blocking collectives  70.9 us (38%)
  waiting for transfers between devices  41 us (22%)
  other arithmetic  28.7 us (15%)
  starting transfers between devices  27.1 us (14%)
  matrix products  9.32 us (5%)
  local copies, waits for them, and re-layouts  8.39 us (4%)
    all_gather x1, blocking collectives, shards(): total = lax.all_gather(over_z, 'z', axis=0, tiled=True)  28.3 us
    all_to_all x1, blocking collectives, spread(): return lax.all_to_all(copies, axes, 0, 0, tiled=True)  22.2 us
    all_gather x2, blocking collectives, right_factor(): summed = jnp.sum(lax.all_gather(pack(product, gram), 'x'), axis=0)  20.4 us
    all_to_all x1, waiting for transfers between devices, shards(): got = lax.all_to_all(sent, ('y', 'core'), 0, 0, tiled=True)  17.8 us
    all_to_all x1, waiting for transfers between devices, shards(): got = lax.all_to_all(sent, 'z', 0, 0, tiled=True)  14.7 us
    another operation x7, other arithmetic, right_factor(): triangle = jnp.linalg.cholesky(gram)  12 us
    all_to_all x1, starting transfers between devices, shards(): got = lax.all_to_all(sent, 'z', 0, 0, tiled=True)  10.5 us
    all_to_all x1, starting transfers between devices, shards(): got = lax.all_to_all(sent, ('y', 'core'), 0, 0, tiled=True)  10.3 us
  transfers between devices with their start and end apart: 3, of which 3 were waited for; matrix products, arithmetic and copies ran while one was open for 0% of the time, Pallas kernels for 0%

profile of v1, /device:TPU:1, one launch (start us, length us, event | category | flops | bytes accessed | tf_op | source)
XLA Modules:
  0.0 186.4 jit_solution(2839647265208039669)
XLA Ops:
  0.6 0.8 convert_element_type.28
  1.5 2.4 %fusion.6 = (bf16[1,2,64,2048]{3,2,1,0:T(8,128)(2,1)}, f32[1,2,64,2048]{3,2,1,0:T(8,128)S(1)}) fusion(bf16[1,2,64,2048]{3,2,1,0:T(8,128)(2,1)} %param.10, bf16[1,2,64,2048]{3,2,1,0:T(8,128)(2,1)} %param.12, bf16[1,2,64,2048]{3,2,1,0:T(8,128)(2,1)} %param.11), kind=kLoop, calls=%fused_computation.13 | loop fusion | flops 1835008 | bytes 3145728 | tf_op jit(solution)/shard_map/convert_element_type | solution.py:43
  3.9 1.0 fusion.4
  6.2 1.8 reshape.62
  8.1 2.4 %pad_maximum_fusion = f32[8,64,640]{2,1,0:T(8,128)} fusion(f32[8,64,64]{2,1,0:T(8,128)S(1)} %bitcast.134, f32[8,64,64]{2,1,0:T(8,128)S(1)} %broadcast_in_dim.38, f32[8,64,512]{2,1,0:T(8,128)} %reshape.62), kind=kLoop, calls=%fused_computation.4 | loop fusion | flops 655360 | bytes 2621440 | tf_op jit(solution)/shard_map/concatenate | solution.py:51
  10.5 10.3 %all-to-all-start = ((f32[8,64,640]{2,1,0:T(8,128)}), f32[8,64,640]{2,1,0:T(8,128)S(1)}, u32[]{:S(2)}, u32[]{:S(2)}) async-start(f32[8,64,640]{2,1,0:T(8,128)} %pad_maximum_fusion), calls=%async_computation | async-start | bytes 2621440 | tf_op jit(solution)/shard_map/all_to_all | solution.py:56
  20.8 17.8 %all-to-all-done = f32[8,64,640]{2,1,0:T(8,128)S(1)} async-done(((f32[8,64,640]{2,1,0:T(8,128)}), f32[8,64,640]{2,1,0:T(8,128)S(1)}, u32[]{:S(2)}, u32[]{:S(2)}) %all-to-all-start) | async-done | bytes 1310752 | tf_op jit(solution)/shard_map/all_to_all | solution.py:56
  38.8 0.8 pad_maximum_fusion.1
  39.7 10.5 %all-to-all-start.1 = ((f32[16,8,640]{2,1,0:T(8,128)}), f32[16,8,640]{2,1,0:T(8,128)S(1)}, u32[]{:S(2)}, u32[]{:S(2)}) async-start(f32[16,8,640]{2,1,0:T(8,128)} %pad_maximum_fusion.1), calls=%async_computation.1 | async-start | bytes 655360 | tf_op jit(solution)/shard_map/all_to_all | solution.py:62
  50.2 14.7 %all-to-all-done.1 = f32[16,8,640]{2,1,0:T(8,128)S(1)} async-done(((f32[16,8,640]{2,1,0:T(8,128)}), f32[16,8,640]{2,1,0:T(8,128)S(1)}, u32[]{:S(2)}, u32[]{:S(2)}) %all-to-all-start.1) | async-done | bytes 327712 | tf_op jit(solution)/shard_map/all_to_all | solution.py:62
  65.0 28.3 %all_gather.15 = f32[128,640]{1,0:T(8,128)S(1)} all-gather(f32[8,640]{1,0:T(8,128)S(1)} %reduce_sum.46), channel_id=1, replica_groups=mesh['y'=4,'z'=16,'x'=4,'core'=2] {'z'}, dimensions={0}, use_global_device_ids=true | all-gather | bytes 348160 | tf_op jit(solution)/shard_map/all_gather | solution.py:66
  94.3 9.8 %all-gather = f32[128,640]{1,0:T(8,128)S(1)} all-gather(f32[32,640]{1,0:T(8,128)S(1)} %fusion.18), channel_id=2, replica_groups=mesh['y'=4,'z'=16,'x'=4,'core'=2] {'x'}, dimensions={0}, use_global_device_ids=true | all-gather | bytes 409600 | tf_op jit(solution)/shard_map/all_gather | solution.py:73
  104.5 5.9 %custom-call.13 = f32[2,32,32]{2,1,0:T(8,128)S(1)} custom-call(f32[2,32,32]{2,1,0:T(8,128)S(1)} %fusion.33), custom_call_target="Cholesky" | custom-call | tf_op jit(solution)/shard_map/jit(cholesky)/cholesky | solution.py:77
  110.6 4.9 %custom-call.14 = f32[2,1,32,32]{2,3,1,0:T(8,128)S(1)} custom-call(f32[2,1,32,32]{3,2,1,0:T(8,128)S(1)} %select_bitcast_fusion), custom_call_target="InvertDiagBlocksLowerTriangular" | custom-call | tf_op jit(solution)/shard_map/vmap(jit(_solve_triangular))/triangular_solve | solution.py:20
  116.5 22.2 %all_to_all.20 = f32[8,64,128]{2,1,0:T(8,128)S(1)} all-to-all(f32[8,64,128]{2,1,0:T(8,128)S(1)} %broadcast_in_dim.42), channel_id=1, replica_groups=mesh['y'=4,'z'=16,'x'=4,'core'=2] {'y','core'}, dimensions={0} | all-to-all | bytes 524288 | tf_op jit(solution)/shard_map/all_to_all | solution.py:16
  139.5 10.6 %all-gather.1 = f32[128,640]{1,0:T(8,128)S(1)} all-gather(f32[32,640]{1,0:T(8,128)S(1)} %select_maximum_fusion), channel_id=3, replica_groups=mesh['y'=4,'z'=16,'x'=4,'core'=2] {'x'}, dimensions={0}, use_global_device_ids=true | all-gather | bytes 409600 | tf_op jit(solution)/shard_map/all_gather | solution.py:73
  150.4 5.9 %custom-call.15 = f32[2,32,32]{2,1,0:T(8,128)S(1)} custom-call(f32[2,32,32]{2,1,0:T(8,128)S(1)} %fusion.31), custom_call_target="Cholesky" | custom-call | tf_op jit(solution)/shard_map/jit(cholesky)/cholesky | solution.py:77
  156.5 4.9 %custom-call.10 = f32[2,1,32,32]{2,3,1,0:T(8,128)S(1)} custom-call(f32[2,1,32,32]{3,2,1,0:T(8,128)S(1)} %fusion.34), custom_call_target="InvertDiagBlocksLowerTriangular" | custom-call | tf_op jit(solution)/shard_map/vmap(jit(_solve_triangular))/triangular_solve | solution.py:20
  161.7 0.8 broadcast_in_dim.43
  162.5 6.3 %all-to-all-start.3 = ((f32[8,2,32,256]{3,2,1,0:T(8,128)}), f32[8,2,32,256]{3,2,1,0:T(8,128)S(1)}, u32[]{:S(2)}, u32[]{:S(2)}) async-start(f32[8,2,32,256]{3,2,1,0:T(8,128)} %broadcast_in_dim.43), calls=%async_computation.3 | async-start | bytes 1048576 | tf_op jit(solution)/shard_map/all_to_all | solution.py:16
  169.7 8.5 %all-to-all-done.3 = f32[8,2,32,256]{3,2,1,0:T(8,128)S(1)} async-done(((f32[8,2,32,256]{3,2,1,0:T(8,128)}), f32[8,2,32,256]{3,2,1,0:T(8,128)S(1)}, u32[]{:S(2)}, u32[]{:S(2)}) %all-to-all-start.3) | async-done | bytes 524320 | tf_op jit(solution)/shard_map/all_to_all | solution.py:16
  178.2 2.0 %copy.127 = f32[2,32,8,256]{1,3,2,0:T(8,128)} copy(f32[2,32,8,256]{3,1,0,2:T(8,128)S(1)} %bitcast.129) | data formatting | bytes 1048576 | tf_op jit(solution)/shard_map/transpose | solution.py:89
  180.1 4.7 %fusion.2 = bf16[1,2,64,2048]{3,2,1,0:T(8,128)(2,1)} fusion(f32[2,32,64]{2,1,0:T(8,128)S(1)} %fusion.27, f32[2,32,2048]{1,2,0:T(8,128)} %bitcast.124, f32[1,2,64,2048]{3,2,1,0:T(8,128)S(1)} %get-tuple-element.31), kind=kOutput, calls=%fused_computation.3 | convolution fusion | flops 101449728 | bytes 2113536 | tf_op jit(solution)/shard_map/mkr,mkd->mrd/dot_general | solution.py:90
  184.9 1.5 fusion.3
  (70 shorter events, 6.5 us)
Async XLA Ops:
  0.6 3.3 %copy-start = (f32[2,32,2048]{2,1,0:T(8,128)S(1)}, f32[2,32,2048]{2,1,0:T(8,128)}, u32[]{:S(2)}) copy-start(f32[2,32,2048]{2,1,0:T(8,128)} %param.13) | copy-start | bytes 1572868
  10.5 28.1 %all-to-all-start = ((f32[8,64,640]{2,1,0:T(8,128)}), f32[8,64,640]{2,1,0:T(8,128)S(1)}, u32[]{:S(2)}, u32[]{:S(2)}) async-start(f32[8,64,640]{2,1,0:T(8,128)} %pad_maximum_fusion), calls=%async_computation | async-start | bytes 2621440 | tf_op jit(solution)/shard_map/all_to_all | solution.py:56
  39.7 25.3 %all-to-all-start.1 = ((f32[16,8,640]{2,1,0:T(8,128)}), f32[16,8,640]{2,1,0:T(8,128)S(1)}, u32[]{:S(2)}, u32[]{:S(2)}) async-start(f32[16,8,640]{2,1,0:T(8,128)} %pad_maximum_fusion.1), calls=%async_computation.1 | async-start | bytes 655360 | tf_op jit(solution)/shard_map/all_to_all | solution.py:62
  150.0 18.8 %copy-start.2 = (f32[2,1,4]{2,1,0:T(1,128)S(1)}, f32[2,1,4]{2,1,0:T(1,128)}, u32[]{:S(2)}) copy-start(f32[2,1,4]{2,1,0:T(1,128)} %param.16) | copy-start | bytes 100
  162.5 15.6 %all-to-all-start.3 = ((f32[8,2,32,256]{3,2,1,0:T(8,128)}), f32[8,2,32,256]{3,2,1,0:T(8,128)S(1)}, u32[]{:S(2)}, u32[]{:S(2)}) async-start(f32[8,2,32,256]{3,2,1,0:T(8,128)} %broadcast_in_dim.43), calls=%async_computation.3 | async-start | bytes 1048576 | tf_op jit(solution)/shard_map/all_to_all | solution.py:16
  180.1 4.7 %copy-start.1 = (f32[2,64,32]{1,2,0:T(8,128)S(1)}, f32[2,64,32]{1,2,0:T(8,128)}, u32[]{:S(2)}) copy-start(f32[2,64,32]{1,2,0:T(8,128)} %param.14) | copy-start | bytes 49156

commit v2 on v1

v2 whole, which is shorter than its diff:
```python
import functools

import jax
import jax.numpy as jnp
from jax import lax
from jax.experimental import pallas as pl
from jax.experimental.pallas import tpu as pltpu
from jax.sharding import Mesh
from jax.sharding import PartitionSpec as P

momentum_decay = 0.9
step_size = 0.5
Y_CHIPS = 4
CORES = 2
LANES = 128
PANEL = 4
STREAMS = ((0, 1),)
HIGH = lax.Precision.HIGHEST
F32 = jnp.float32


def dot(left, right, left_dim, right_dim):
    dims = (((left_dim,), (right_dim,)), ((), ()))
    return lax.dot_general(left, right, dims, precision=HIGH, preferred_element_type=F32)


def call(kernel, outs, *args, in_specs=None, out_specs=None, aliases=None):
    vmem = pl.BlockSpec(memory_space=pltpu.VMEM)
    return pl.pallas_call(
        kernel,
        out_shape=outs,
        in_specs=in_specs or [vmem] * len(args),
        out_specs=out_specs or jax.tree.map(lambda _: vmem, outs),
        input_output_aliases=aliases or {},
    )(*args)


def shape(*dims, dtype=F32):
    return jax.ShapeDtypeStruct(dims, dtype)


def iota(dims, axis):
    return lax.broadcasted_iota(jnp.int32, dims, axis)


def unrounded(moment, grad, error, m):
    moment_f = momentum_decay * moment[0, m].astype(F32) + grad[0, m].astype(F32)
    return moment_f + error[0, m].astype(F32)


def first_kernel(mats, groups, grad, error, moment, dirs, norm, sent):
    rows, width = grad.shape[2:]
    cols = width // groups
    rank = dirs.shape[1]
    at = len(mats) * cols
    sent[:, :, at:] = jnp.zeros((groups, rows, LANES), F32)
    for i, m in enumerate(mats):
        values = unrounded(moment, grad, error, m)
        for j in range(groups):
            sent[j, :, i * cols : (i + 1) * cols] = values[:, j * cols : (j + 1) * cols]
        factor = dot(values, dirs[m], 1, 1)
        for j in range(groups):
            sent[j, :, at + i * rank : at + (i + 1) * rank] = factor
    n_mat, per_tensor = norm.shape
    features = per_tensor // (groups // CORES)
    terms = norm[...].astype(F32)
    for j in range(groups):
        start = (j // CORES) * features
        sent[j, 0:n_mat, at + LANES // 2 : at + LANES // 2 + features] = terms[:, start : start + features]


def write_products(mats, cols, rank, matrix, factor, out):
    count = len(mats)
    grams = None
    lane = iota((rank, count * rank), 1)
    for i in range(count):
        own = factor[:, i * rank : (i + 1) * rank]
        product = dot(own, matrix[:, i * cols : (i + 1) * cols], 0, 0)
        gram = dot(own, factor, 0, 0)
        grams = gram if grams is None else jnp.where(lane >= i * rank, gram, grams)
        for j in range(out.shape[0]):
            out[j, :, i * cols : (i + 1) * cols] = product
    for j in range(out.shape[0]):
        out[j, :, count * cols :] = jnp.zeros((rank, LANES), F32)
        out[j, :, count * cols : count * (cols + rank)] = grams


def product_kernel(mats, cols, rank, matrix, out):
    count = len(mats)
    factor = matrix[:, count * cols : count * (cols + rank)]
    write_products(mats, cols, rank, matrix, factor, out)


def unpack_kernel(mats, cols, rank, matrix, got, out, factor_out):
    count = len(mats)
    summed = jnp.sum(got[...], axis=0)
    pieces = LANES // (count * rank)
    height = summed.shape[0]
    for j in range(pieces):
        factor_out[j * height : (j + 1) * height, :] = summed[:, j * count * rank : (j + 1) * count * rank]
    write_products(mats, cols, rank, matrix, factor_out[...], out)


def inverse_factors(a, count, rank):
    dims = a.shape
    row = iota(dims, 0)
    place = (iota(dims, 1) // rank) % count
    pivots = jnp.ones(dims, F32)
    for p in range(0, rank, PANEL):
        columns, lines = [], []
        for j in range(p, p + PANEL):
            column = jnp.broadcast_to(a[:, j : j + 1], dims)
            for i in range(1, count):
                other = jnp.broadcast_to(a[:, i * rank + j : i * rank + j + 1], dims)
                column = jnp.where(place == i, other, column)
            columns.append(column)
            lines.append(a[j : j + 1, :])
        for j in range(PANEL):
            pivot = columns[j][p + j : p + j + 1, :]
            times = jnp.where(row > p + j, columns[j], 0.0) * (1.0 / pivot)
            a = a - times * lines[j]
            pivots = jnp.where(row == p + j, pivot, pivots)
            for q in range(j + 1, PANEL):
                columns[q] = columns[q] - times * columns[j][p + q : p + q + 1, :]
                lines[q] = lines[q] - times[p + q : p + q + 1, :] * lines[j]
    scaled = a * (1.0 / jnp.sqrt(pivots))
    at = count * rank
    return [scaled[:, at + i * rank : at + (i + 1) * rank] for i in range(count)]


def solved(mats, cols, rank, got):
    count = len(mats)
    summed = jnp.sum(got[...], axis=0)
    a = summed[:, count * cols :]
    lane, row = iota(a.shape, 1), iota(a.shape, 0)
    at = count * rank
    one = (lane >= at) & (lane < 2 * at) & (lane % rank == row)
    inverses = inverse_factors(jnp.where(one, 1.0, a), count, rank)
    return inverses, [dot(inverses[i], summed[:, i * cols : (i + 1) * cols], 1, 0) for i in range(count)]


def left_kernel(mats, cols, rank, got, matrix, out):
    count = len(mats)
    _, directions = solved(mats, cols, rank, got)
    height = out.shape[1]
    for i in range(count):
        factor = dot(matrix[:, i * cols : (i + 1) * cols], directions[i], 1, 1)
        for piece in range(LANES // (count * rank)):
            part = factor[piece * height : (piece + 1) * height, :]
            start = (piece * count + i) * rank
            for j in range(out.shape[0]):
                out[j, :, start : start + rank] = part


def right_kernel(mats, cols, rank, rows, core, got, factor, out, basis):
    inverses, directions = solved(mats, cols, rank, got)
    start = pl.multiple_of(core[0] * rows, rows)
    own = factor[pl.ds(start, rows), :]
    for i in range(len(mats)):
        for j in range(out.shape[0]):
            out[j, i * rank : (i + 1) * rank, :] = directions[i]
        basis[i] = dot(own[:, i * rank : (i + 1) * rank], inverses[i], 1, 1)


def last_kernel(mats, replicas, rank, place, got, basis, grad, error, moment, weight, *refs):
    new_error, new_weight = refs[-2:]
    cols = got.shape[2]
    weight_cols = weight.shape[1]
    for i, m in enumerate(mats):
        values = unrounded(moment, grad, error, m)
        left = basis[i]
        for j in range(got.shape[0]):
            approx = dot(left, got[j, i * rank : (i + 1) * rank, :], 1, 0) / replicas
            part = values[:, j * cols : (j + 1) * cols] - approx
            new_error[0, i, :, j * cols : (j + 1) * cols] = part.astype(jnp.bfloat16)
        own = got[place[0], i * rank : (i + 1) * rank, :]
        own = pltpu.roll(own, place[1], 1)[:, :LANES]
        approx = dot(own, left, 0, 1) / replicas
        new_weight[i] = weight[m] - step_size * approx[:weight_cols, :]


def exchange(value, axes):
    return lax.all_to_all(value, axes, 0, 0, tiled=True)


def shards(grad_kv, error_kv, moment_kv, start_dirs, weight_kv, norm_grads, norm_gains):
    n_y, n_z, n_x, n_core = (lax.axis_size(a) for a in ("y", "z", "x", "core"))
    replicas = n_y * n_z
    y, z, core = (lax.axis_index(a) for a in ("y", "z", "core"))
    _, n_mat, rows, width = grad_kv.shape
    rank = start_dirs.shape[1]
    groups = n_y * n_core
    cols = width // groups
    chip_rows = rows * n_core
    z_rows = chip_rows // n_z
    gain_cols = norm_gains.shape[2]
    weight_cols = weight_kv.shape[2]
    weight_t = jnp.swapaxes(weight_kv, 1, 2)
    smem = pl.BlockSpec(memory_space=pltpu.SMEM)
    vmem = pl.BlockSpec(memory_space=pltpu.VMEM)
    core_at = core[None]
    column = (y * n_z + z) * weight_cols
    place = jnp.stack([column // cols, (cols - column % cols) % cols])

    moment_f = momentum_decay * moment_kv.astype(F32) + grad_kv.astype(F32)
    new_moment_kv = moment_f.astype(jnp.bfloat16)

    new_gains, errors, weights = None, [], []
    for mats in STREAMS:
        count = len(mats)
        lanes = count * cols + LANES
        at = count * cols
        norm_at = at + LANES // 2
        sent = call(
            functools.partial(first_kernel, mats, groups),
            shape(groups, rows, lanes),
            grad_kv, error_kv, moment_kv, start_dirs, norm_grads[0],
        )
        got = exchange(sent, ("y", "core"))
        over_y = jnp.sum(got.reshape(n_y, n_core, rows, lanes), axis=0)
        norm_y = lax.dynamic_index_in_dim(over_y, core, 0, keepdims=False)[:z_rows, norm_at:]
        norm_y = jnp.broadcast_to(norm_y[None], (n_z, z_rows, LANES // 2))
        sent = jnp.concatenate([over_y.reshape(n_z, z_rows, lanes)[:, :, :norm_at], norm_y], axis=2)
        over_z = jnp.sum(exchange(sent, "z"), axis=0)
        if new_gains is None:
            own_norm = lax.dynamic_slice(over_z, (0, norm_at + z * gain_cols), (n_mat, gain_cols))
            new_gains = norm_gains - step_size * (own_norm / replicas)[:, None, :]
        copies = jnp.broadcast_to(over_z[None], (n_z, z_rows, lanes))
        matrix = exchange(copies, "z").reshape(chip_rows, lanes)

        sizes = (mats, cols, rank)
        height = chip_rows * count * rank // LANES
        products = call(functools.partial(product_kernel, *sizes), shape(n_x, rank, lanes), matrix)
        got = exchange(products, "x")
        factors = call(functools.partial(left_kernel, *sizes), shape(groups, height, LANES), got, matrix)
        got = exchange(factors, ("y", "core"))
        products, factor = call(
            functools.partial(unpack_kernel, *sizes),
            (shape(n_x, rank, lanes), shape(chip_rows, count * rank)),
            matrix, got,
        )
        got = exchange(products, "x")
        directions, basis = call(
            functools.partial(right_kernel, *sizes, rows),
            (shape(groups, count * rank, cols), shape(count, rows, rank)),
            core_at, got, factor,
            in_specs=[smem, vmem, vmem],
        )
        got = exchange(directions, ("y", "core"))
        error, weight = call(
            functools.partial(last_kernel, mats, replicas, rank),
            (shape(1, count, rows, width, dtype=jnp.bfloat16), shape(count, weight_cols, rows)),
            place, got, basis, grad_kv, error_kv, moment_kv, weight_t,
            in_specs=[smem] + [vmem] * 6,
        )
        errors.append(error)
        weights.append(weight)
    new_error_kv = jnp.concatenate(errors, axis=1)
    new_weight_kv = jnp.swapaxes(jnp.concatenate(weights, axis=0), 1, 2)
    return (new_weight_kv, new_error_kv, new_moment_kv, new_gains)


def solution(mesh):
    dp, tensor = mesh.devices.shape
    sizes = (Y_CHIPS, dp // Y_CHIPS, tensor // CORES, CORES)
    chips = Mesh(mesh.devices.reshape(sizes), ("y", "z", "x", "core"))
    dp, tensor = ("y", "z"), ("x", "core")
    return jax.shard_map(
        shards,
        mesh=chips,
        in_specs=(
            P(dp, None, tensor, None),
            P(dp, None, tensor, None),
            P(dp, None, tensor, None),
            P(),
            P(None, tensor, dp),
            P(dp, None, tensor),
            P(None, tensor, dp),
        ),
        out_specs=(
            P(None, tensor, dp),
            P(dp, None, tensor, None),
            P(dp, None, tensor, None),
            P(None, tensor, dp),
        ),
        check_vma=False,
    )
```

time: 187 us -> 155 us (0.83)
  other arithmetic: 28.7 us -> 2.4 us
  blocking collectives: 70.9 us -> 91 us
  Pallas kernels: 0 us -> 18.1 us
  waiting for transfers between devices: 41 us -> 25 us
  starting transfers between devices: 27.1 us -> 16 us
  matrix products: 9.32 us -> 0 us
  local copies, waits for them, and re-layouts: 8.39 us -> 0.92 us
    all_to_all x1 -> x5, blocking collectives: 22.2 us -> 91 us  [exchange(): return lax.all_to_all(value, axes, 0, 0, tiled=True)]
    all_gather x3 -> x0, blocking collectives: 48.7 us -> none  [the longest x1 28.3 us: shards(): total = lax.all_gather(over_z, 'z', axis=0, tiled=True)]
    another operation x14 -> x1, other arithmetic: 22.1 us -> 0.61 us  [shards(): place = jnp.stack([column // cols, (cols - column % cols) % cols])]
    pallas_call x0 -> x6, Pallas kernels: none -> 18.1 us  [call(): pl.pallas_call(kernel, out_shape=outs, in_specs=in_specs or [vmem] * len(...]
    all_to_all x3 -> x2, waiting for transfers between devices: 41 us -> 25 us  [exchange(): return lax.all_to_all(value, axes, 0, 0, tiled=True)]
    all_to_all x3 -> x2, starting transfers between devices: 27.1 us -> 16 us  [exchange(): return lax.all_to_all(value, axes, 0, 0, tiled=True)]
    dot_general x8 -> x0, matrix products: 8.52 us -> none  [the longest x1 4.72 us: shards(): jnp.einsum('mkr,mkd->mrd', basis_t, directions, precision=HIGH) / replicas]
    concatenate x4 -> x1, other arithmetic: 3.42 us -> 0.09 us  [shards(): jnp.concatenate([over_y.reshape(n_z, z_rows, lanes)[:, :, :norm_at], norm...]
  transfers between devices with their start and end apart: 3 -> 2, of which waited for: 3 -> 2; matrix products, arithmetic and copies ran while one was open for 0% -> 1% of each run, Pallas kernels for 0% -> 0%
where the time goes in v2:
time: 155 us; the launch traced here: 154 us
  blocking collectives  91 us (59%)
  waiting for transfers between devices  25 us (16%)
  Pallas kernels  18.1 us (12%)
  starting transfers between devices  16 us (10%)
  other arithmetic  2.4 us (2%)
    all_to_all x5, blocking collectives, exchange(): return lax.all_to_all(value, axes, 0, 0, tiled=True)  91 us
    all_to_all x2, waiting for transfers between devices, exchange(): return lax.all_to_all(value, axes, 0, 0, tiled=True)  25 us
    pallas_call x6, Pallas kernels, call(): pl.pallas_call(kernel, out_shape=outs, in_specs=in_specs or [vmem] * len(...  18.1 us
    all_to_all x2, starting transfers between devices, exchange(): return lax.all_to_all(value, axes, 0, 0, tiled=True)  16 us
  transfers between devices with their start and end apart: 2, of which 2 were waited for; matrix products, arithmetic and copies ran while one was open for 1% of the time, Pallas kernels for 0%

profile of v2, /device:TPU:1, one launch (start us, length us, event | category | flops | bytes accessed | tf_op | source)
XLA Modules:
  0.0 154.1 jit_solution(13039528545874479332)
XLA Ops:
  0.6 3.6 %shard_map.102 = f32[8,64,640]{2,1,0:T(8,128)} custom-call(bf16[1,2,64,2048]{3,2,1,0:T(8,128)(2,1)} %grad.3, bf16[1,2,64,2048]{3,2,1,0:T(8,128)(2,1)} %error.3, bf16[1,2,64,2048]{3,2,1,0:T(8,128)(2,1)} %moment.3, f32[2,32,2048]{2,1,0:T(8,128)} %dirs.1, bf16[2,256]{1,0:T(2,128)(2,1)} %bitcast.22), custom_call_target="tpu_custom_call" | custom-call | tf_op jit(solution)/shard_map/pallas_call | solution.py:29
  4.3 10.3 %all-to-all-start = ((f32[8,64,640]{2,1,0:T(8,128)}), f32[8,64,640]{2,1,0:T(8,128)S(1)}, u32[]{:S(2)}, u32[]{:S(2)}) async-start(f32[8,64,640]{2,1,0:T(8,128)} %shard_map.102), calls=%async_computation | async-start | bytes 2621440 | tf_op jit(solution)/shard_map/all_to_all | solution.py:183
  14.6 17.8 %all-to-all-done = f32[8,64,640]{2,1,0:T(8,128)S(1)} async-done(((f32[8,64,640]{2,1,0:T(8,128)}), f32[8,64,640]{2,1,0:T(8,128)S(1)}, u32[]{:S(2)}, u32[]{:S(2)}) %all-to-all-start) | async-done | bytes 1310752 | tf_op jit(solution)/shard_map/all_to_all | solution.py:183
  32.4 0.1 reduce_sum.18
  32.5 0.1 slice.9
  32.6 0.1 pad_maximum_fusion
  32.7 25.1 %all_to_all.35 = f32[16,8,640]{2,1,0:T(8,128)S(1)} all-to-all(f32[16,8,640]{2,1,0:T(8,128)S(1)} %pad_maximum_fusion), channel_id=1, replica_groups=mesh['y'=4,'z'=16,'x'=4,'core'=2] {'z'}, dimensions={0} | all-to-all | bytes 655360 | tf_op jit(solution)/shard_map/all_to_all | solution.py:183
  57.8 27.3 %all_to_all.36 = f32[16,8,640]{2,1,0:T(8,128)} all-to-all(f32[16,8,640]{2,1,0:T(8,128)S(1)} %broadcast_in_dim.8), channel_id=1, replica_groups=mesh['y'=4,'z'=16,'x'=4,'core'=2] {'z'}, dimensions={0} | all-to-all | bytes 655360 | tf_op jit(solution)/shard_map/all_to_all | solution.py:183
  85.1 2.1 %shard_map.103 = f32[4,32,640]{2,1,0:T(8,128)} custom-call(f32[128,640]{1,0:T(8,128)} %bitcast.17), custom_call_target="tpu_custom_call" | custom-call | tf_op jit(solution)/shard_map/pallas_call | solution.py:29
  87.2 10.0 %all_to_all.37.got = f32[4,32,640]{2,1,0:T(8,128)} all-to-all(f32[4,32,640]{2,1,0:T(8,128)} %shard_map.103), channel_id=1, replica_groups=mesh['y'=4,'z'=16,'x'=4,'core'=2] {'x'}, dimensions={0} | all-to-all | bytes 655360 | tf_op jit(solution)/shard_map/all_to_all | solution.py:183
  97.2 3.5 %shard_map.104 = f32[8,64,128]{2,1,0:T(8,128)} custom-call(f32[4,32,640]{2,1,0:T(8,128)} %all_to_all.37.got, f32[128,640]{1,0:T(8,128)} %bitcast.18), custom_call_target="tpu_custom_call" | custom-call | tf_op jit(solution)/shard_map/pallas_call | solution.py:29
  100.8 18.3 %all_to_all.38.got = f32[8,64,128]{2,1,0:T(8,128)} all-to-all(f32[8,64,128]{2,1,0:T(8,128)} %shard_map.104), channel_id=1, replica_groups=mesh['y'=4,'z'=16,'x'=4,'core'=2] {'y','core'}, dimensions={0} | all-to-all | bytes 524288 | tf_op jit(solution)/shard_map/all_to_all | solution.py:183
  119.1 2.3 %shard_map.105 = (f32[4,32,640]{2,1,0:T(8,128)}, f32[128,64]{1,0:T(8,128)}) custom-call(f32[128,640]{1,0:T(8,128)} %bitcast.19, f32[8,64,128]{2,1,0:T(8,128)} %all_to_all.38.got), custom_call_target="tpu_custom_call" | custom-call | tf_op jit(solution)/shard_map/pallas_call | solution.py:29
  121.4 10.3 %all_to_all.39.got = f32[4,32,640]{2,1,0:T(8,128)} all-to-all(f32[4,32,640]{2,1,0:T(8,128)} %get-tuple-element.10), channel_id=1, replica_groups=mesh['y'=4,'z'=16,'x'=4,'core'=2] {'x'}, dimensions={0} | all-to-all | bytes 655360 | tf_op jit(solution)/shard_map/all_to_all | solution.py:183
  131.7 3.1 %shard_map.106 = (f32[8,64,256]{2,1,0:T(8,128)}, f32[2,64,32]{2,1,0:T(8,128)}) custom-call(s32[1]{0:T(128)} %bitcast.2.core, f32[4,32,640]{2,1,0:T(8,128)} %all_to_all.39.got, f32[128,64]{1,0:T(8,128)} %get-tuple-element.11.factor), custom_call_target="tpu_custom_call" | custom-call | tf_op jit(solution)/shard_map/pallas_call | solution.py:29
  134.8 5.7 %all-to-all-start.6 = ((f32[8,64,256]{2,1,0:T(8,128)}), f32[8,64,256]{2,1,0:T(8,128)S(1)}, u32[]{:S(2)}, u32[]{:S(2)}) async-start(f32[8,64,256]{2,1,0:T(8,128)} %get-tuple-element.12), calls=%async_computation.6 | async-start | bytes 1048576 | tf_op jit(solution)/shard_map/all_to_all | solution.py:183
  140.5 0.0 copy-done
  140.5 0.0 copy-done.1
  140.5 1.0 add_convert_fusion
  141.5 0.6 pad_add_fusion.place
  142.1 0.6 bitcast_subtract_fusion
  142.7 7.2 %all-to-all-done.6.got = f32[8,64,256]{2,1,0:T(8,128)S(1)} async-done(((f32[8,64,256]{2,1,0:T(8,128)}), f32[8,64,256]{2,1,0:T(8,128)S(1)}, u32[]{:S(2)}, u32[]{:S(2)}) %all-to-all-start.6) | async-done | bytes 524320 | tf_op jit(solution)/shard_map/all_to_all | solution.py:183
  149.9 0.8 copy-done.2
  150.7 3.4 %shard_map.107 = (bf16[1,2,64,2048]{3,2,1,0:T(8,128)(2,1)}, f32[2,32,64]{2,1,0:T(8,128)}) custom-call(s32[2]{0:T(128)} %pad_add_fusion.place, f32[8,64,256]{2,1,0:T(8,128)} %copy-done.2, f32[2,64,32]{2,1,0:T(8,128)} %get-tuple-element.13.basis, bf16[1,2,64,2048]{3,2,1,0:T(8,128)(2,1)} %grad.3, bf16[1,2,64,2048]{3,2,1,0:T(8,128)(2,1)} %error.3, ...), custom_call_target="tpu_custom_call" | custom-call | tf_op jit(solution)/shard_map/pallas_call | solution.py:29
  (9 shorter events, 0.1 us)
Async XLA Ops:
  4.3 28.1 %all-to-all-start = ((f32[8,64,640]{2,1,0:T(8,128)}), f32[8,64,640]{2,1,0:T(8,128)S(1)}, u32[]{:S(2)}, u32[]{:S(2)}) async-start(f32[8,64,640]{2,1,0:T(8,128)} %shard_map.102), calls=%async_computation | async-start | bytes 2621440 | tf_op jit(solution)/shard_map/all_to_all | solution.py:183
  119.1 21.4 %copy-start = (bf16[1,2,64,2048]{3,2,1,0:T(8,128)(2,1)S(1)}, bf16[1,2,64,2048]{3,2,1,0:T(8,128)(2,1)}, u32[]{:S(2)}) copy-start(bf16[1,2,64,2048]{3,2,1,0:T(8,128)(2,1)} %grad.3) | copy-start | bytes 1572868
  119.1 21.4 %copy-start.1 = (bf16[1,2,64,2048]{3,2,1,0:T(8,128)(2,1)S(1)}, bf16[1,2,64,2048]{3,2,1,0:T(8,128)(2,1)}, u32[]{:S(2)}) copy-start(bf16[1,2,64,2048]{3,2,1,0:T(8,128)(2,1)} %moment.3) | copy-start | bytes 1572868
  134.8 7.3 %copy-start.3 = (f32[2,1,4]{2,1,0:T(1,128)S(1)}, f32[2,1,4]{2,1,0:T(1,128)}, u32[]{:S(2)}) copy-start(f32[2,1,4]{2,1,0:T(1,128)} %param.13) | copy-start | bytes 100
  134.8 15.1 %all-to-all-start.6 = ((f32[8,64,256]{2,1,0:T(8,128)}), f32[8,64,256]{2,1,0:T(8,128)S(1)}, u32[]{:S(2)}, u32[]{:S(2)}) async-start(f32[8,64,256]{2,1,0:T(8,128)} %get-tuple-element.12), calls=%async_computation.6 | async-start | bytes 1048576 | tf_op jit(solution)/shard_map/all_to_all | solution.py:183
  149.9 0.8 copy-start.2

commit v3 on v2

--- a/solution.py
+++ b/solution.py
@@ -37,6 +37,14 @@
 
 def shape(*dims, dtype=F32):
     return jax.ShapeDtypeStruct(dims, dtype)
+
+
+def local(*dims):
+    return pltpu.VMEM(dims, F32)
+
+
+def keep(value):
+    return pltpu.with_memory_space_constraint(value, pltpu.VMEM)
 
 
 def iota(dims, axis):
@@ -180,7 +188,7 @@
 
 
 def exchange(value, axes):
-    return lax.all_to_all(value, axes, 0, 0, tiled=True)
+    return keep(lax.all_to_all(value, axes, 0, 0, tiled=True))
 
 
 def shards(grad_kv, error_kv, moment_kv, start_dirs, weight_kv, norm_grads, norm_gains):
@@ -213,44 +221,45 @@
         norm_at = at + LANES // 2
         sent = call(
             functools.partial(first_kernel, mats, groups),
-            shape(groups, rows, lanes),
+            local(groups, rows, lanes),
             grad_kv, error_kv, moment_kv, start_dirs, norm_grads[0],
         )
-        got = exchange(sent, ("y", "core"))
+        got = lax.all_to_all(sent, ("y", "core"), 0, 0, tiled=True)
         over_y = jnp.sum(got.reshape(n_y, n_core, rows, lanes), axis=0)
         norm_y = lax.dynamic_index_in_dim(over_y, core, 0, keepdims=False)[:z_rows, norm_at:]
         norm_y = jnp.broadcast_to(norm_y[None], (n_z, z_rows, LANES // 2))
         sent = jnp.concatenate([over_y.reshape(n_z, z_rows, lanes)[:, :, :norm_at], norm_y], axis=2)
-        over_z = jnp.sum(exchange(sent, "z"), axis=0)
+        over_z = jnp.sum(lax.all_to_all(sent, "z", 0, 0, tiled=True), axis=0)
         if new_gains is None:
             own_norm = lax.dynamic_slice(over_z, (0, norm_at + z * gain_cols), (n_mat, gain_cols))
             new_gains = norm_gains - step_size * (own_norm / replicas)[:, None, :]
         copies = jnp.broadcast_to(over_z[None], (n_z, z_rows, lanes))
-        matrix = exchange(copies, "z").reshape(chip_rows, lanes)
+        matrix = lax.all_to_all(copies, "z", 0, 0, tiled=True)
+        matrix = keep(matrix.reshape(chip_rows, lanes))
 
         sizes = (mats, cols, rank)
         height = chip_rows * count * rank // LANES
-        products = call(functools.partial(product_kernel, *sizes), shape(n_x, rank, lanes), matrix)
+        products = call(functools.partial(product_kernel, *sizes), local(n_x, rank, lanes), matrix)
         got = exchange(products, "x")
-        factors = call(functools.partial(left_kernel, *sizes), shape(groups, height, LANES), got, matrix)
+        factors = call(functools.partial(left_kernel, *sizes), local(groups, height, LANES), got, matrix)
         got = exchange(factors, ("y", "core"))
         products, factor = call(
             functools.partial(unpack_kernel, *sizes),
-            (shape(n_x, rank, lanes), shape(chip_rows, count * rank)),
+            (local(n_x, rank, lanes), local(chip_rows, count * rank)),
             matrix, got,
         )
         got = exchange(products, "x")
         directions, basis = call(
             functools.partial(right_kernel, *sizes, rows),
-            (shape(groups, count * rank, cols), shape(count, rows, rank)),
-            core_at, got, factor,
+            (local(groups, count * rank, cols), local(count, rows, rank)),
+            core_at, got, keep(factor),
             in_specs=[smem, vmem, vmem],
         )
         got = exchange(directions, ("y", "core"))
         error, weight = call(
             functools.partial(last_kernel, mats, replicas, rank),
             (shape(1, count, rows, width, dtype=jnp.bfloat16), shape(count, weight_cols, rows)),
-            place, got, basis, grad_kv, error_kv, moment_kv, weight_t,
+            place, got, keep(basis), grad_kv, error_kv, moment_kv, weight_t,
             in_specs=[smem] + [vmem] * 6,
         )
         errors.append(error)

time: 155 us -> 144 us (0.929)
  Pallas kernels: 18.1 us -> 11.6 us
  blocking collectives: 91 us -> 87.2 us
    pallas_call x6, Pallas kernels: 18.1 us -> 11.6 us  [call(): pl.pallas_call(kernel, out_shape=outs, in_specs=in_specs or [vmem] * len(...]
    all_to_all x5, blocking collectives: 91 us -> 87.2 us  [the longest x3 34.9 us: exchange(): return keep(lax.all_to_all(value, axes, 0, 0, tiled=True))]
  transfers between devices with their start and end apart: 2 -> 2, of which waited for: 2 -> 2; matrix products, arithmetic and copies ran while one was open for 1% -> 2% of each run, Pallas kernels for 0% -> 0%
where the time goes in v3:
time: 144 us; the launch traced here: 143 us
  blocking collectives  87.2 us (61%)
  waiting for transfers between devices  25 us (17%)
  starting transfers between devices  16 us (11%)
  Pallas kernels  11.6 us (8%)
  other arithmetic  2.38 us (2%)
    all_to_all x3, blocking collectives, exchange(): return keep(lax.all_to_all(value, axes, 0, 0, tiled=True))  34.9 us
    all_to_all x1, blocking collectives, shards(): matrix = lax.all_to_all(copies, 'z', 0, 0, tiled=True)  27.2 us
    all_to_all x1, blocking collectives, shards(): over_z = jnp.sum(lax.all_to_all(sent, 'z', 0, 0, tiled=True), axis=0)  25.1 us
    all_to_all x1, waiting for transfers between devices, shards(): got = lax.all_to_all(sent, ('y', 'core'), 0, 0, tiled=True)  17.8 us
    pallas_call x6, Pallas kernels, call(): pl.pallas_call(kernel, out_shape=outs, in_specs=in_specs or [vmem] * len(...  11.6 us
    all_to_all x1, starting transfers between devices, shards(): got = lax.all_to_all(sent, ('y', 'core'), 0, 0, tiled=True)  10.3 us
    all_to_all x1, waiting for transfers between devices, exchange(): return keep(lax.all_to_all(value, axes, 0, 0, tiled=True))  7.19 us
    all_to_all x1, starting transfers between devices, exchange(): return keep(lax.all_to_all(value, axes, 0, 0, tiled=True))  5.72 us
  transfers between devices with their start and end apart: 2, of which 2 were waited for; matrix products, arithmetic and copies ran while one was open for 2% of the time, Pallas kernels for 0%

profile of v3, /device:TPU:1, one launch (start us, length us, event | category | flops | bytes accessed | tf_op | source)
XLA Modules:
  0.0 143.0 jit_solution(17492273148697933123)
XLA Ops:
  0.6 3.6 %shard_map.102 = f32[8,64,640]{2,1,0:T(8,128)} custom-call(bf16[1,2,64,2048]{3,2,1,0:T(8,128)(2,1)} %grad.3, bf16[1,2,64,2048]{3,2,1,0:T(8,128)(2,1)} %error.3, bf16[1,2,64,2048]{3,2,1,0:T(8,128)(2,1)} %moment.3, f32[2,32,2048]{2,1,0:T(8,128)} %dirs.1, bf16[2,256]{1,0:T(2,128)(2,1)} %bitcast.22), custom_call_target="tpu_custom_call" | custom-call | tf_op jit(solution)/shard_map/pallas_call | solution.py:29
  4.3 10.3 %all-to-all-start = ((f32[8,64,640]{2,1,0:T(8,128)}), f32[8,64,640]{2,1,0:T(8,128)S(1)}, u32[]{:S(2)}, u32[]{:S(2)}) async-start(f32[8,64,640]{2,1,0:T(8,128)} %shard_map.102), calls=%async_computation | async-start | bytes 2621440 | tf_op jit(solution)/shard_map/all_to_all | solution.py:227
  14.6 17.8 %all-to-all-done = f32[8,64,640]{2,1,0:T(8,128)S(1)} async-done(((f32[8,64,640]{2,1,0:T(8,128)}), f32[8,64,640]{2,1,0:T(8,128)S(1)}, u32[]{:S(2)}, u32[]{:S(2)}) %all-to-all-start) | async-done | bytes 1310752 | tf_op jit(solution)/shard_map/all_to_all | solution.py:227
  32.4 0.1 reduce_sum.18
  32.5 0.1 slice.9
  32.6 0.1 pad_maximum_fusion
  32.7 25.1 %all_to_all.35 = f32[16,8,640]{2,1,0:T(8,128)S(1)} all-to-all(f32[16,8,640]{2,1,0:T(8,128)S(1)} %pad_maximum_fusion), channel_id=1, replica_groups=mesh['y'=4,'z'=16,'x'=4,'core'=2] {'z'}, dimensions={0} | all-to-all | bytes 655360 | tf_op jit(solution)/shard_map/all_to_all | solution.py:232
  57.8 27.2 %all_to_all.36 = f32[16,8,640]{2,1,0:T(8,128)S(1)} all-to-all(f32[16,8,640]{2,1,0:T(8,128)S(1)} %broadcast_in_dim.8), channel_id=1, replica_groups=mesh['y'=4,'z'=16,'x'=4,'core'=2] {'z'}, dimensions={0} | all-to-all | bytes 655360 | tf_op jit(solution)/shard_map/all_to_all | solution.py:237
  85.0 0.4 shard_map.103
  85.4 9.7 %all_to_all.37.got = f32[4,32,640]{2,1,0:T(8,128)S(1)} all-to-all(f32[4,32,640]{2,1,0:T(8,128)S(1)} %shard_map.103), channel_id=1, replica_groups=mesh['y'=4,'z'=16,'x'=4,'core'=2] {'x'}, dimensions={0} | all-to-all | bytes 655360 | tf_op jit(solution)/shard_map/all_to_all | solution.py:191
  95.1 1.8 %shard_map.104 = f32[8,64,128]{2,1,0:T(8,128)S(1)} custom-call(f32[4,32,640]{2,1,0:T(8,128)S(1)} %all_to_all.37.got, f32[128,640]{1,0:T(8,128)S(1)} %bitcast.17), custom_call_target="tpu_custom_call" | custom-call | tf_op jit(solution)/shard_map/pallas_call | solution.py:29
  96.8 16.8 %all_to_all.38.got = f32[8,64,128]{2,1,0:T(8,128)S(1)} all-to-all(f32[8,64,128]{2,1,0:T(8,128)S(1)} %shard_map.104), channel_id=1, replica_groups=mesh['y'=4,'z'=16,'x'=4,'core'=2] {'y','core'}, dimensions={0} | all-to-all | bytes 524288 | tf_op jit(solution)/shard_map/all_to_all | solution.py:191
  113.6 0.4 shard_map.105
  114.1 8.5 %all_to_all.39.got = f32[4,32,640]{2,1,0:T(8,128)S(1)} all-to-all(f32[4,32,640]{2,1,0:T(8,128)S(1)} %get-tuple-element.10), channel_id=1, replica_groups=mesh['y'=4,'z'=16,'x'=4,'core'=2] {'x'}, dimensions={0} | all-to-all | bytes 655360 | tf_op jit(solution)/shard_map/all_to_all | solution.py:191
  122.6 2.1 %shard_map.106 = (f32[8,64,256]{2,1,0:T(8,128)}, f32[2,64,32]{2,1,0:T(8,128)S(1)}) custom-call(s32[1]{0:T(128)} %bitcast.2.core, f32[4,32,640]{2,1,0:T(8,128)S(1)} %all_to_all.39.got, f32[128,64]{1,0:T(8,128)S(1)} %get-tuple-element.11.factor), custom_call_target="tpu_custom_call" | custom-call | tf_op jit(solution)/shard_map/pallas_call | solution.py:29
  124.7 5.7 %all-to-all-start.6 = ((f32[8,64,256]{2,1,0:T(8,128)}), f32[8,64,256]{2,1,0:T(8,128)S(1)}, u32[]{:S(2)}, u32[]{:S(2)}) async-start(f32[8,64,256]{2,1,0:T(8,128)} %get-tuple-element.12), calls=%async_computation.6 | async-start | bytes 1048576 | tf_op jit(solution)/shard_map/all_to_all | solution.py:191
  130.4 0.0 copy-done
  130.4 0.0 copy-done.1
  130.4 1.0 add_convert_fusion
  131.4 0.6 pad_add_fusion.place
  132.0 0.0 copy-done.2
  132.0 0.6 bitcast_subtract_fusion
  132.6 7.2 %all-to-all-done.6.got = f32[8,64,256]{2,1,0:T(8,128)S(1)} async-done(((f32[8,64,256]{2,1,0:T(8,128)}), f32[8,64,256]{2,1,0:T(8,128)S(1)}, u32[]{:S(2)}, u32[]{:S(2)}) %all-to-all-start.6) | async-done | bytes 524320 | tf_op jit(solution)/shard_map/all_to_all | solution.py:191
  139.8 3.2 %shard_map.107 = (bf16[1,2,64,2048]{3,2,1,0:T(8,128)(2,1)}, f32[2,32,64]{2,1,0:T(8,128)}) custom-call(s32[2]{0:T(128)} %pad_add_fusion.place, f32[8,64,256]{2,1,0:T(8,128)S(1)} %all-to-all-done.6.got, f32[2,64,32]{2,1,0:T(8,128)S(1)} %get-tuple-element.13.basis, bf16[1,2,64,2048]{3,2,1,0:T(8,128)(2,1)} %grad.3, bf16[1,2,64,2048]{3,2,1,0:T(8,128)(2,1)} %error.3, ...), custom_call_target="tpu_custom_call" | custom-call | tf_op jit(solution)/shard_map/pallas_call | solution.py:29
  (7 shorter events, 0.1 us)
Async XLA Ops:
  4.3 28.1 %all-to-all-start = ((f32[8,64,640]{2,1,0:T(8,128)}), f32[8,64,640]{2,1,0:T(8,128)S(1)}, u32[]{:S(2)}, u32[]{:S(2)}) async-start(f32[8,64,640]{2,1,0:T(8,128)} %shard_map.102), calls=%async_computation | async-start | bytes 2621440 | tf_op jit(solution)/shard_map/all_to_all | solution.py:227
  113.6 16.8 %copy-start = (bf16[1,2,64,2048]{3,2,1,0:T(8,128)(2,1)S(1)}, bf16[1,2,64,2048]{3,2,1,0:T(8,128)(2,1)}, u32[]{:S(2)}) copy-start(bf16[1,2,64,2048]{3,2,1,0:T(8,128)(2,1)} %grad.3) | copy-start | bytes 1572868
  113.6 16.8 %copy-start.1 = (bf16[1,2,64,2048]{3,2,1,0:T(8,128)(2,1)S(1)}, bf16[1,2,64,2048]{3,2,1,0:T(8,128)(2,1)}, u32[]{:S(2)}) copy-start(bf16[1,2,64,2048]{3,2,1,0:T(8,128)(2,1)} %moment.3) | copy-start | bytes 1572868
  124.7 7.3 %copy-start.2 = (f32[2,1,4]{2,1,0:T(1,128)S(1)}, f32[2,1,4]{2,1,0:T(1,128)}, u32[]{:S(2)}) copy-start(f32[2,1,4]{2,1,0:T(1,128)} %param.13) | copy-start | bytes 100
  124.7 15.1 %all-to-all-start.6 = ((f32[8,64,256]{2,1,0:T(8,128)}), f32[8,64,256]{2,1,0:T(8,128)S(1)}, u32[]{:S(2)}, u32[]{:S(2)}) async-start(f32[8,64,256]{2,1,0:T(8,128)} %get-tuple-element.12), calls=%async_computation.6 | async-start | bytes 1048576 | tf_op jit(solution)/shard_map/all_to_all | solution.py:191

commit v4 on v3

--- a/solution.py
+++ b/solution.py
@@ -12,6 +12,7 @@
 step_size = 0.5
 Y_CHIPS = 4
 CORES = 2
+PAIR = 2
 LANES = 128
 PANEL = 4
 STREAMS = ((0, 1),)
@@ -56,25 +57,34 @@
     return moment_f + error[0, m].astype(F32)
 
 
-def first_kernel(mats, groups, grad, error, moment, dirs, norm, sent):
+def first_kernel(mats, groups, block, grad, error, moment, dirs, norm, sent):
     rows, width = grad.shape[2:]
     cols = width // groups
     rank = dirs.shape[1]
     at = len(mats) * cols
-    sent[:, :, at:] = jnp.zeros((groups, rows, LANES), F32)
+    total, height = sent.shape[:2]
+    sent[:, :, at:] = jnp.zeros((total, height, LANES), F32)
+    places = [(j, zl, q) for j in range(groups) for zl in range(PAIR) for q in range(height // block)]
+
+    def dest(j, zl):
+        return (j // CORES * PAIR + zl) * CORES + j % CORES
+
     for i, m in enumerate(mats):
         values = unrounded(moment, grad, error, m)
-        for j in range(groups):
-            sent[j, :, i * cols : (i + 1) * cols] = values[:, j * cols : (j + 1) * cols]
         factor = dot(values, dirs[m], 1, 1)
-        for j in range(groups):
-            sent[j, :, at + i * rank : at + (i + 1) * rank] = factor
+        for j, zl, q in places:
+            start = (q * PAIR + zl) * block
+            own = slice(q * block, (q + 1) * block)
+            sent[dest(j, zl), own, i * cols : (i + 1) * cols] = values[start : start + block, j * cols : (j + 1) * cols]
+            sent[dest(j, zl), own, at + i * rank : at + (i + 1) * rank] = factor[start : start + block, :]
     n_mat, per_tensor = norm.shape
     features = per_tensor // (groups // CORES)
     terms = norm[...].astype(F32)
     for j in range(groups):
         start = (j // CORES) * features
-        sent[j, 0:n_mat, at + LANES // 2 : at + LANES // 2 + features] = terms[:, start : start + features]
+        for zl in range(PAIR):
+            lane = at + LANES // 2
+            sent[dest(j, zl), 0:n_mat, lane : lane + features] = terms[:, start : start + features]
 
 
 def write_products(mats, cols, rank, matrix, factor, out):
@@ -170,18 +180,23 @@
         basis[i] = dot(own[:, i * rank : (i + 1) * rank], inverses[i], 1, 1)
 
 
-def last_kernel(mats, replicas, rank, place, got, basis, grad, error, moment, weight, *refs):
-    new_error, new_weight = refs[-2:]
+def last_kernel(mats, replicas, rank, place, got, other, basis, grad, error, moment, weight, new_error, new_weight):
     cols = got.shape[2]
     weight_cols = weight.shape[1]
+    first, same = place[2] == 0, place[3] == 1
     for i, m in enumerate(mats):
         values = unrounded(moment, grad, error, m)
         left = basis[i]
-        for j in range(got.shape[0]):
-            approx = dot(left, got[j, i * rank : (i + 1) * rank, :], 1, 0) / replicas
-            part = values[:, j * cols : (j + 1) * cols] - approx
-            new_error[0, i, :, j * cols : (j + 1) * cols] = part.astype(jnp.bfloat16)
-        own = got[place[0], i * rank : (i + 1) * rank, :]
+        own_rank = slice(i * rank, (i + 1) * rank)
+        for y in range(got.shape[0]):
+            mine, theirs = got[y, own_rank, :], other[y, own_rank, :]
+            for c in range(CORES):
+                right = jnp.where(first, *((mine, theirs) if c == 0 else (theirs, mine)))
+                approx = dot(left, right, 1, 0) / replicas
+                start = (y * CORES + c) * cols
+                part = values[:, start : start + cols] - approx
+                new_error[0, i, :, start : start + cols] = part.astype(jnp.bfloat16)
+        own = jnp.where(same, got[place[0], own_rank, :], other[place[0], own_rank, :])
         own = pltpu.roll(own, place[1], 1)[:, :LANES]
         approx = dot(own, left, 0, 1) / replicas
         new_weight[i] = weight[m] - step_size * approx[:weight_cols, :]
@@ -192,9 +207,11 @@
 
 
 def shards(grad_kv, error_kv, moment_kv, start_dirs, weight_kv, norm_grads, norm_gains):
-    n_y, n_z, n_x, n_core = (lax.axis_size(a) for a in ("y", "z", "x", "core"))
+    n_y, n_zh, n_zl, n_x, n_core = (lax.axis_size(a) for a in ("y", "zh", "zl", "x", "core"))
+    n_z = n_zh * n_zl
     replicas = n_y * n_z
-    y, z, core = (lax.axis_index(a) for a in ("y", "z", "core"))
+    y, core = lax.axis_index("y"), lax.axis_index("core")
+    z = lax.axis_index("zh") * n_zl + lax.axis_index("zl")
     _, n_mat, rows, width = grad_kv.shape
     rank = start_dirs.shape[1]
     groups = n_y * n_core
@@ -208,7 +225,9 @@
     vmem = pl.BlockSpec(memory_space=pltpu.VMEM)
     core_at = core[None]
     column = (y * n_z + z) * weight_cols
-    place = jnp.stack([column // cols, (cols - column % cols) % cols])
+    group = column // cols
+    same = (group % n_core == core).astype(jnp.int32)
+    place = jnp.stack([group // n_core, (cols - column % cols) % cols, core, same])
 
     moment_f = momentum_decay * moment_kv.astype(F32) + grad_kv.astype(F32)
     new_moment_kv = moment_f.astype(jnp.bfloat16)
@@ -220,21 +239,21 @@
         at = count * cols
         norm_at = at + LANES // 2
         sent = call(
-            functools.partial(first_kernel, mats, groups),
-            local(groups, rows, lanes),
+            functools.partial(first_kernel, mats, groups, z_rows),
+            local(groups * n_zl, rows // n_zl, lanes),
             grad_kv, error_kv, moment_kv, start_dirs, norm_grads[0],
         )
-        got = lax.all_to_all(sent, ("y", "core"), 0, 0, tiled=True)
-        over_y = jnp.sum(got.reshape(n_y, n_core, rows, lanes), axis=0)
+        got = lax.all_to_all(sent, ("y", "zl", "core"), 0, 0, tiled=True)
+        over_y = jnp.sum(got.reshape(n_y * n_zl, n_core, rows // n_zl, lanes), axis=0)
         norm_y = lax.dynamic_index_in_dim(over_y, core, 0, keepdims=False)[:z_rows, norm_at:]
-        norm_y = jnp.broadcast_to(norm_y[None], (n_z, z_rows, LANES // 2))
-        sent = jnp.concatenate([over_y.reshape(n_z, z_rows, lanes)[:, :, :norm_at], norm_y], axis=2)
-        over_z = jnp.sum(lax.all_to_all(sent, "z", 0, 0, tiled=True), axis=0)
+        norm_y = jnp.broadcast_to(norm_y[None], (n_zh, z_rows, LANES // 2))
+        sent = jnp.concatenate([over_y.reshape(n_zh, z_rows, lanes)[:, :, :norm_at], norm_y], axis=2)
+        over_z = jnp.sum(lax.all_to_all(sent, "zh", 0, 0, tiled=True), axis=0)
         if new_gains is None:
             own_norm = lax.dynamic_slice(over_z, (0, norm_at + z * gain_cols), (n_mat, gain_cols))
             new_gains = norm_gains - step_size * (own_norm / replicas)[:, None, :]
         copies = jnp.broadcast_to(over_z[None], (n_z, z_rows, lanes))
-        matrix = lax.all_to_all(copies, "z", 0, 0, tiled=True)
+        matrix = lax.all_to_all(copies, ("zh", "zl"), 0, 0, tiled=True)
         matrix = keep(matrix.reshape(chip_rows, lanes))
 
         sizes = (mats, cols, rank)
@@ -251,16 +270,17 @@
         got = exchange(products, "x")
         directions, basis = call(
             functools.partial(right_kernel, *sizes, rows),
-            (local(groups, count * rank, cols), local(count, rows, rank)),
+            (local(n_y, count * rank, cols), local(count, rows, rank)),
             core_at, got, keep(factor),
             in_specs=[smem, vmem, vmem],
         )
-        got = exchange(directions, ("y", "core"))
+        got = exchange(directions, "y")
+        other = keep(lax.ppermute(got, "core", [(i, n_core - 1 - i) for i in range(n_core)]))
         error, weight = call(
             functools.partial(last_kernel, mats, replicas, rank),
             (shape(1, count, rows, width, dtype=jnp.bfloat16), shape(count, weight_cols, rows)),
-            place, got, keep(basis), grad_kv, error_kv, moment_kv, weight_t,
-            in_specs=[smem] + [vmem] * 6,
+            place, got, other, keep(basis), keep(grad_kv), keep(error_kv), keep(moment_kv), weight_t,
+            in_specs=[smem] + [vmem] * 7,
         )
         errors.append(error)
         weights.append(weight)
@@ -271,9 +291,9 @@
 
 def solution(mesh):
     dp, tensor = mesh.devices.shape
-    sizes = (Y_CHIPS, dp // Y_CHIPS, tensor // CORES, CORES)
-    chips = Mesh(mesh.devices.reshape(sizes), ("y", "z", "x", "core"))
-    dp, tensor = ("y", "z"), ("x", "core")
+    sizes = (Y_CHIPS, dp // Y_CHIPS // PAIR, PAIR, tensor // CORES, CORES)
+    chips = Mesh(mesh.devices.reshape(sizes), ("y", "zh", "zl", "x", "core"))
+    dp, tensor = ("y", "zh", "zl"), ("x", "core")
     return jax.shard_map(
         shards,
         mesh=chips,

time: 144 us -> 138 us (0.958)
  blocking collectives: 87.2 us -> 80.8 us
  starting transfers between devices: 16 us -> 19 us
  waiting for transfers between devices: 25 us -> 23.1 us
    all_to_all x2, blocking collectives: 52.3 us -> 45.4 us  [the longest x1 24.8 us: shards(): over_z = jnp.sum(lax.all_to_all(sent, 'zh', 0, 0, tiled=True), axis=0)]
    ppermute x0 -> x1, starting transfers between devices: none -> 5.24 us  [shards(): lax.ppermute(got, 'core', [(i, n_core - 1 - i) for i in range(n_core)])]
    all_to_all x1, waiting for transfers between devices: 7.19 us -> 4.52 us  [exchange(): return keep(lax.all_to_all(value, axes, 0, 0, tiled=True))]
    all_to_all x1, starting transfers between devices: 5.72 us -> 3.41 us  [exchange(): return keep(lax.all_to_all(value, axes, 0, 0, tiled=True))]
  transfers between devices with their start and end apart: 2 -> 3, of which waited for: 2 -> 2; matrix products, arithmetic and copies ran while one was open for 2% -> 2% of each run, Pallas kernels for 0% -> 0%
where the time goes in v4:
time: 138 us; the launch traced here: 137 us
  blocking collectives  80.8 us (59%)
  waiting for transfers between devices  23.1 us (17%)
  starting transfers between devices  19 us (14%)
  Pallas kernels  10.9 us (8%)
  other arithmetic  2.42 us (2%)
    all_to_all x3, blocking collectives, exchange(): return keep(lax.all_to_all(value, axes, 0, 0, tiled=True))  35.4 us
    all_to_all x1, blocking collectives, shards(): over_z = jnp.sum(lax.all_to_all(sent, 'zh', 0, 0, tiled=True), axis=0)  24.8 us
    all_to_all x1, blocking collectives, shards(): matrix = lax.all_to_all(copies, ('zh', 'zl'), 0, 0, tiled=True)  20.6 us
    all_to_all x1, waiting for transfers between devices, shards(): got = lax.all_to_all(sent, ('y', 'zl', 'core'), 0, 0, tiled=True)  18.6 us
    pallas_call x6, Pallas kernels, call(): pl.pallas_call(kernel, out_shape=outs, in_specs=in_specs or [vmem] * len(...  10.9 us
    all_to_all x1, starting transfers between devices, shards(): got = lax.all_to_all(sent, ('y', 'zl', 'core'), 0, 0, tiled=True)  10.3 us
    ppermute x1, starting transfers between devices, shards(): lax.ppermute(got, 'core', [(i, n_core - 1 - i) for i in range(n_core)])  5.24 us
    all_to_all x1, waiting for transfers between devices, exchange(): return keep(lax.all_to_all(value, axes, 0, 0, tiled=True))  4.52 us
  transfers between devices with their start and end apart: 3, of which 2 were waited for; matrix products, arithmetic and copies ran while one was open for 2% of the time, Pallas kernels for 0%

profile of v4, /device:TPU:1, one launch (start us, length us, event | category | flops | bytes accessed | tf_op | source)
XLA Modules:
  0.0 137.0 jit_solution(9808830556313900247)
XLA Ops:
  0.6 3.7 %shard_map.102 = f32[16,32,640]{2,1,0:T(8,128)} custom-call(bf16[1,2,64,2048]{3,2,1,0:T(8,128)(2,1)} %grad.3, bf16[1,2,64,2048]{3,2,1,0:T(8,128)(2,1)} %error.3, bf16[1,2,64,2048]{3,2,1,0:T(8,128)(2,1)} %moment.3, f32[2,32,2048]{2,1,0:T(8,128)} %dirs.1, bf16[2,256]{1,0:T(2,128)(2,1)} %bitcast.23), custom_call_target="tpu_custom_call" | custom-call | tf_op jit(solution)/shard_map/pallas_call | solution.py:30
  4.3 10.3 %all-to-all-start = ((f32[16,32,640]{2,1,0:T(8,128)}), f32[16,32,640]{2,1,0:T(8,128)S(1)}, u32[]{:S(2)}, u32[]{:S(2)}) async-start(f32[16,32,640]{2,1,0:T(8,128)} %shard_map.102), calls=%async_computation | async-start | bytes 2621440 | tf_op jit(solution)/shard_map/all_to_all | solution.py:246
  14.6 18.6 %all-to-all-done = f32[16,32,640]{2,1,0:T(8,128)S(1)} async-done(((f32[16,32,640]{2,1,0:T(8,128)}), f32[16,32,640]{2,1,0:T(8,128)S(1)}, u32[]{:S(2)}, u32[]{:S(2)}) %all-to-all-start) | async-done | bytes 1310752 | tf_op jit(solution)/shard_map/all_to_all | solution.py:246
  33.2 0.1 reduce_sum.18
  33.3 0.1 slice.9
  33.4 0.1 pad_maximum_fusion
  33.5 24.8 %all_to_all.35 = f32[8,8,640]{2,1,0:T(8,128)S(1)} all-to-all(f32[8,8,640]{2,1,0:T(8,128)S(1)} %pad_maximum_fusion), channel_id=1, replica_groups=mesh['y'=4,'zh'=8,'zl'=2,'x'=4,'core'=2] {'zh'}, dimensions={0} | all-to-all | bytes 327680 | tf_op jit(solution)/shard_map/all_to_all | solution.py:251
  58.3 20.6 %all_to_all.36 = f32[16,8,640]{2,1,0:T(8,128)S(1)} all-to-all(f32[16,8,640]{2,1,0:T(8,128)S(1)} %broadcast_in_dim.5), channel_id=1, replica_groups=mesh['y'=4,'zh'=8,'zl'=2,'x'=4,'core'=2] {'zh','zl'}, dimensions={0} | all-to-all | bytes 655360 | tf_op jit(solution)/shard_map/all_to_all | solution.py:256
  78.9 0.4 shard_map.103
  79.3 9.7 %all_to_all.37.got = f32[4,32,640]{2,1,0:T(8,128)S(1)} all-to-all(f32[4,32,640]{2,1,0:T(8,128)S(1)} %shard_map.103), channel_id=1, replica_groups=mesh['y'=4,'zh'=8,'zl'=2,'x'=4,'core'=2] {'x'}, dimensions={0} | all-to-all | bytes 655360 | tf_op jit(solution)/shard_map/all_to_all | solution.py:206
  89.0 1.8 %shard_map.104 = f32[8,64,128]{2,1,0:T(8,128)S(1)} custom-call(f32[4,32,640]{2,1,0:T(8,128)S(1)} %all_to_all.37.got, f32[128,640]{1,0:T(8,128)S(1)} %bitcast.18), custom_call_target="tpu_custom_call" | custom-call | tf_op jit(solution)/shard_map/pallas_call | solution.py:30
  90.8 0.0 copy-start
  90.8 0.0 copy-start.1
  90.8 17.2 %all_to_all.38.got = f32[8,64,128]{2,1,0:T(8,128)S(1)} all-to-all(f32[8,64,128]{2,1,0:T(8,128)S(1)} %shard_map.104), channel_id=1, replica_groups=mesh['y'=4,'zh'=8,'zl'=2,'x'=4,'core'=2] {'y','core'}, dimensions={0} | all-to-all | bytes 524288 | tf_op jit(solution)/shard_map/all_to_all | solution.py:206
  108.0 0.4 shard_map.105
  108.4 8.5 %all_to_all.39.got = f32[4,32,640]{2,1,0:T(8,128)S(1)} all-to-all(f32[4,32,640]{2,1,0:T(8,128)S(1)} %get-tuple-element.10), channel_id=1, replica_groups=mesh['y'=4,'zh'=8,'zl'=2,'x'=4,'core'=2] {'x'}, dimensions={0} | all-to-all | bytes 655360 | tf_op jit(solution)/shard_map/all_to_all | solution.py:206
  117.0 2.0 %shard_map.106 = (f32[4,64,256]{2,1,0:T(8,128)}, f32[2,64,32]{2,1,0:T(8,128)S(1)}) custom-call(s32[1]{0:T(128)} %bitcast.2.core, f32[4,32,640]{2,1,0:T(8,128)S(1)} %all_to_all.39.got, f32[128,64]{1,0:T(8,128)S(1)} %get-tuple-element.11.factor), custom_call_target="tpu_custom_call" | custom-call | tf_op jit(solution)/shard_map/pallas_call | solution.py:30
  119.0 3.4 %all-to-all-start.6 = ((f32[4,64,256]{2,1,0:T(8,128)}), f32[4,64,256]{2,1,0:T(8,128)S(1)}, u32[]{:S(2)}, u32[]{:S(2)}) async-start(f32[4,64,256]{2,1,0:T(8,128)} %get-tuple-element.12), calls=%async_computation.6 | async-start | bytes 524288 | tf_op jit(solution)/shard_map/all_to_all | solution.py:206
  122.4 1.0 add_convert_fusion
  123.3 4.5 %all-to-all-done.6.got = f32[4,64,256]{2,1,0:T(8,128)S(1)} async-done(((f32[4,64,256]{2,1,0:T(8,128)}), f32[4,64,256]{2,1,0:T(8,128)S(1)}, u32[]{:S(2)}, u32[]{:S(2)}) %all-to-all-start.6) | async-done | bytes 262176 | tf_op jit(solution)/shard_map/all_to_all | solution.py:206
  127.9 5.2 %collective-permute-start = (f32[4,64,256]{2,1,0:T(8,128)S(1)}, f32[4,64,256]{2,1,0:T(8,128)S(1)}, u32[]{:S(2)}, u32[]{:S(2)}) collective-permute-start(f32[4,64,256]{2,1,0:T(8,128)S(1)} %all-to-all-done.6.got), channel_id=1, source_target_pairs={{0,1},{1,0},{2,3},{3,2},{4,5},{5,4},{6,7},{7,6},{8,9},{9,8},{10,11... | collective-permute-start | bytes 786440 | tf_op jit(solution)/shard_map/ppermute | solution.py:278
  133.1 0.7 pad_add_fusion.place
  133.8 0.6 bitcast_subtract_fusion
  134.4 2.6 %shard_map.107 = (bf16[1,2,64,2048]{3,2,1,0:T(8,128)(2,1)}, f32[2,32,64]{2,1,0:T(8,128)}) custom-call(s32[4]{0:T(128)} %pad_add_fusion.place, f32[4,64,256]{2,1,0:T(8,128)S(1)} %all-to-all-done.6.got, f32[4,64,256]{2,1,0:T(8,128)S(1)} %collective-permute-done.other, f32[2,64,32]{2,1,0:T(8,128)S(1)} %get-tuple-element.13.basis, ...), custom_call_target="tpu_custom_call" | custom-call | tf_op jit(solution)/shard_map/pallas_call | solution.py:30
  (11 shorter events, 0.1 us)
Async XLA Ops:
  4.3 28.9 %all-to-all-start = ((f32[16,32,640]{2,1,0:T(8,128)}), f32[16,32,640]{2,1,0:T(8,128)S(1)}, u32[]{:S(2)}, u32[]{:S(2)}) async-start(f32[16,32,640]{2,1,0:T(8,128)} %shard_map.102), calls=%async_computation | async-start | bytes 2621440 | tf_op jit(solution)/shard_map/all_to_all | solution.py:246
  90.8 31.6 %copy-start = (bf16[1,2,64,2048]{3,2,1,0:T(8,128)(2,1)S(1)}, bf16[1,2,64,2048]{3,2,1,0:T(8,128)(2,1)}, u32[]{:S(2)}) copy-start(bf16[1,2,64,2048]{3,2,1,0:T(8,128)(2,1)} %grad.3) | copy-start | bytes 1572868
  90.8 31.6 %copy-start.1 = (bf16[1,2,64,2048]{3,2,1,0:T(8,128)(2,1)S(1)}, bf16[1,2,64,2048]{3,2,1,0:T(8,128)(2,1)}, u32[]{:S(2)}) copy-start(bf16[1,2,64,2048]{3,2,1,0:T(8,128)(2,1)} %moment.3) | copy-start | bytes 1572868
  117.0 16.8 %copy-start.3 = (f32[2,1,4]{2,1,0:T(1,128)S(1)}, f32[2,1,4]{2,1,0:T(1,128)}, u32[]{:S(2)}) copy-start(f32[2,1,4]{2,1,0:T(1,128)} %param.13) | copy-start | bytes 100
  117.0 17.5 %copy-start.2 = (bf16[1,2,64,2048]{3,2,1,0:T(8,128)(2,1)S(1)}, bf16[1,2,64,2048]{3,2,1,0:T(8,128)(2,1)}, u32[]{:S(2)}) copy-start(bf16[1,2,64,2048]{3,2,1,0:T(8,128)(2,1)} %error.3) | copy-start | bytes 1572868
  119.0 8.9 %all-to-all-start.6 = ((f32[4,64,256]{2,1,0:T(8,128)}), f32[4,64,256]{2,1,0:T(8,128)S(1)}, u32[]{:S(2)}, u32[]{:S(2)}) async-start(f32[4,64,256]{2,1,0:T(8,128)} %get-tuple-element.12), calls=%async_computation.6 | async-start | bytes 524288 | tf_op jit(solution)/shard_map/all_to_all | solution.py:206
  127.9 6.5 %collective-permute-start = (f32[4,64,256]{2,1,0:T(8,128)S(1)}, f32[4,64,256]{2,1,0:T(8,128)S(1)}, u32[]{:S(2)}, u32[]{:S(2)}) collective-permute-start(f32[4,64,256]{2,1,0:T(8,128)S(1)} %all-to-all-done.6.got), channel_id=1, source_target_pairs={{0,1},{1,0},{2,3},{3,2},{4,5},{5,4},{6,7},{7,6},{8,9},{9,8},{10,11... | collective-permute-start | bytes 786440 | tf_op jit(solution)/shard_map/ppermute | solution.py:278

commit v5 on v4

--- a/solution.py
+++ b/solution.py
@@ -223,12 +223,6 @@
     weight_t = jnp.swapaxes(weight_kv, 1, 2)
     smem = pl.BlockSpec(memory_space=pltpu.SMEM)
     vmem = pl.BlockSpec(memory_space=pltpu.VMEM)
-    core_at = core[None]
-    column = (y * n_z + z) * weight_cols
-    group = column // cols
-    same = (group % n_core == core).astype(jnp.int32)
-    place = jnp.stack([group // n_core, (cols - column % cols) % cols, core, same])
-
     moment_f = momentum_decay * moment_kv.astype(F32) + grad_kv.astype(F32)
     new_moment_kv = moment_f.astype(jnp.bfloat16)
 
@@ -243,7 +237,14 @@
             local(groups * n_zl, rows // n_zl, lanes),
             grad_kv, error_kv, moment_kv, start_dirs, norm_grads[0],
         )
+        sent, indices = lax.optimization_barrier((sent, (y, z, core)))
         got = lax.all_to_all(sent, ("y", "zl", "core"), 0, 0, tiled=True)
+        got, (y, z, core) = lax.optimization_barrier((got, indices))
+        core_at = core[None]
+        column = (y * n_z + z) * weight_cols
+        group = column // cols
+        same = (group % n_core == core).astype(jnp.int32)
+        place = jnp.stack([group // n_core, (cols - column % cols) % cols, core, same])
         over_y = jnp.sum(got.reshape(n_y * n_zl, n_core, rows // n_zl, lanes), axis=0)
         norm_y = lax.dynamic_index_in_dim(over_y, core, 0, keepdims=False)[:z_rows, norm_at:]
         norm_y = jnp.broadcast_to(norm_y[None], (n_zh, z_rows, LANES // 2))

time: 138 us -> 136 us (0.986)
  blocking collectives: 80.8 us -> 109 us
  waiting for transfers between devices: 23.1 us -> 4.52 us
  starting transfers between devices: 19 us -> 8.65 us
    all_to_all x0 -> x1, blocking collectives: none -> 27.8 us  [shards(): got = lax.all_to_all(sent, ('y', 'zl', 'core'), 0, 0, tiled=True)]
    all_to_all x1 -> x0, waiting for transfers between devices: 18.6 us -> none  [shards(): got = lax.all_to_all(sent, ('y', 'zl', 'core'), 0, 0, tiled=True)]
    all_to_all x1 -> x0, starting transfers between devices: 10.3 us -> none  [shards(): got = lax.all_to_all(sent, ('y', 'zl', 'core'), 0, 0, tiled=True)]
  transfers between devices with their start and end apart: 3 -> 2, of which waited for: 2 -> 1; matrix products, arithmetic and copies ran while one was open for 2% -> 2% of each run, Pallas kernels for 0% -> 0%
where the time goes in v5:
time: 136 us
  blocking collectives  109 us (80%)
  Pallas kernels  9.8 us (7%)
  starting transfers between devices  8.65 us (6%)
  waiting for transfers between devices  4.52 us (3%)
  other arithmetic  2.43 us (2%)
    all_to_all x3, blocking collectives, exchange(): return keep(lax.all_to_all(value, axes, 0, 0, tiled=True))  35.6 us
    all_to_all x1, blocking collectives, shards(): got = lax.all_to_all(sent, ('y', 'zl', 'core'), 0, 0, tiled=True)  27.8 us
    all_to_all x1, blocking collectives, shards(): over_z = jnp.sum(lax.all_to_all(sent, 'zh', 0, 0, tiled=True), axis=0)  26.1 us
    all_to_all x1, blocking collectives, shards(): matrix = lax.all_to_all(copies, ('zh', 'zl'), 0, 0, tiled=True)  19.9 us
    pallas_call x6, Pallas kernels, call(): pl.pallas_call(kernel, out_shape=outs, in_specs=in_specs or [vmem] * len(...  9.8 us
    ppermute x1, starting transfers between devices, shards(): lax.ppermute(got, 'core', [(i, n_core - 1 - i) for i in range(n_core)])  5.24 us
    all_to_all x1, waiting for transfers between devices, exchange(): return keep(lax.all_to_all(value, axes, 0, 0, tiled=True))  4.52 us
    all_to_all x1, starting transfers between devices, exchange(): return keep(lax.all_to_all(value, axes, 0, 0, tiled=True))  3.41 us
  transfers between devices with their start and end apart: 2, of which 1 were waited for; matrix products, arithmetic and copies ran while one was open for 2% of the time, Pallas kernels for 0%

profile of v5, /device:TPU:1, one launch (start us, length us, event | category | flops | bytes accessed | tf_op | source)
XLA Modules:
  0.0 135.7 jit_solution(15955453920278310896)
XLA Ops:
  0.6 2.6 %shard_map.102 = f32[16,32,640]{2,1,0:T(8,128)S(1)} custom-call(bf16[1,2,64,2048]{3,2,1,0:T(8,128)(2,1)} %grad.3, bf16[1,2,64,2048]{3,2,1,0:T(8,128)(2,1)} %error.3, bf16[1,2,64,2048]{3,2,1,0:T(8,128)(2,1)} %moment.3, f32[2,32,2048]{2,1,0:T(8,128)} %dirs.1, bf16[2,256]{1,0:T(2,128)(2,1)} %bitcast.23), custom_call_target="tpu_custom_call" | custom-call | tf_op jit(solution)/shard_map/pallas_call | solution.py:30
  3.2 27.8 %all_to_all.35 = f32[16,32,640]{2,1,0:T(8,128)S(1)} all-to-all(f32[16,32,640]{2,1,0:T(8,128)S(1)} %shard_map.102), channel_id=1, replica_groups=mesh['y'=4,'zh'=8,'zl'=2,'x'=4,'core'=2] {'y','zl','core'}, dimensions={0} | all-to-all | bytes 2621440 | tf_op jit(solution)/shard_map/all_to_all | solution.py:241
  31.0 0.1 reduce_sum.18
  31.1 0.1 slice.9
  31.2 0.1 pad_maximum_fusion
  31.2 26.1 %all_to_all.36 = f32[8,8,640]{2,1,0:T(8,128)S(1)} all-to-all(f32[8,8,640]{2,1,0:T(8,128)S(1)} %pad_maximum_fusion), channel_id=1, replica_groups=mesh['y'=4,'zh'=8,'zl'=2,'x'=4,'core'=2] {'zh'}, dimensions={0} | all-to-all | bytes 327680 | tf_op jit(solution)/shard_map/all_to_all | solution.py:252
  57.4 19.9 %all_to_all.37 = f32[16,8,640]{2,1,0:T(8,128)S(1)} all-to-all(f32[16,8,640]{2,1,0:T(8,128)S(1)} %broadcast_in_dim.5), channel_id=1, replica_groups=mesh['y'=4,'zh'=8,'zl'=2,'x'=4,'core'=2] {'zh','zl'}, dimensions={0} | all-to-all | bytes 655360 | tf_op jit(solution)/shard_map/all_to_all | solution.py:257
  77.4 0.4 shard_map.103
  77.8 9.7 %all_to_all.38.got = f32[4,32,640]{2,1,0:T(8,128)S(1)} all-to-all(f32[4,32,640]{2,1,0:T(8,128)S(1)} %shard_map.103), channel_id=1, replica_groups=mesh['y'=4,'zh'=8,'zl'=2,'x'=4,'core'=2] {'x'}, dimensions={0} | all-to-all | bytes 655360 | tf_op jit(solution)/shard_map/all_to_all | solution.py:206
  87.5 1.8 %shard_map.104 = f32[8,64,128]{2,1,0:T(8,128)S(1)} custom-call(f32[4,32,640]{2,1,0:T(8,128)S(1)} %all_to_all.38.got, f32[128,640]{1,0:T(8,128)S(1)} %bitcast.18), custom_call_target="tpu_custom_call" | custom-call | tf_op jit(solution)/shard_map/pallas_call | solution.py:30
  89.2 0.0 copy-start
  89.3 0.0 copy-start.1
  89.3 17.4 %all_to_all.39.got = f32[8,64,128]{2,1,0:T(8,128)S(1)} all-to-all(f32[8,64,128]{2,1,0:T(8,128)S(1)} %shard_map.104), channel_id=1, replica_groups=mesh['y'=4,'zh'=8,'zl'=2,'x'=4,'core'=2] {'y','core'}, dimensions={0} | all-to-all | bytes 524288 | tf_op jit(solution)/shard_map/all_to_all | solution.py:206
  106.7 0.4 shard_map.105
  107.1 8.5 %all_to_all.40.got = f32[4,32,640]{2,1,0:T(8,128)S(1)} all-to-all(f32[4,32,640]{2,1,0:T(8,128)S(1)} %get-tuple-element.26), channel_id=1, replica_groups=mesh['y'=4,'zh'=8,'zl'=2,'x'=4,'core'=2] {'x'}, dimensions={0} | all-to-all | bytes 655360 | tf_op jit(solution)/shard_map/all_to_all | solution.py:206
  115.6 2.0 %shard_map.106 = (f32[4,64,256]{2,1,0:T(8,128)}, f32[2,64,32]{2,1,0:T(8,128)S(1)}) custom-call(s32[1]{0:T(128)} %bitcast.3.core, f32[4,32,640]{2,1,0:T(8,128)S(1)} %all_to_all.40.got, f32[128,64]{1,0:T(8,128)S(1)} %get-tuple-element.27.factor), custom_call_target="tpu_custom_call" | custom-call | tf_op jit(solution)/shard_map/pallas_call | solution.py:30
  117.6 3.4 %all-to-all-start.6 = ((f32[4,64,256]{2,1,0:T(8,128)}), f32[4,64,256]{2,1,0:T(8,128)S(1)}, u32[]{:S(2)}, u32[]{:S(2)}) async-start(f32[4,64,256]{2,1,0:T(8,128)} %get-tuple-element.28), calls=%async_computation.6 | async-start | bytes 524288 | tf_op jit(solution)/shard_map/all_to_all | solution.py:206
  121.1 1.0 add_convert_fusion
  122.0 4.5 %all-to-all-done.6.got = f32[4,64,256]{2,1,0:T(8,128)S(1)} async-done(((f32[4,64,256]{2,1,0:T(8,128)}), f32[4,64,256]{2,1,0:T(8,128)S(1)}, u32[]{:S(2)}, u32[]{:S(2)}) %all-to-all-start.6) | async-done | bytes 262176 | tf_op jit(solution)/shard_map/all_to_all | solution.py:206
  126.6 5.2 %collective-permute-start = (f32[4,64,256]{2,1,0:T(8,128)S(1)}, f32[4,64,256]{2,1,0:T(8,128)S(1)}, u32[]{:S(2)}, u32[]{:S(2)}) collective-permute-start(f32[4,64,256]{2,1,0:T(8,128)S(1)} %all-to-all-done.6.got), channel_id=1, source_target_pairs={{0,1},{1,0},{2,3},{3,2},{4,5},{5,4},{6,7},{7,6},{8,9},{9,8},{10,11... | collective-permute-start | bytes 786440 | tf_op jit(solution)/shard_map/ppermute | solution.py:279
  131.8 0.7 pad_add_fusion.place
  132.5 0.6 bitcast_subtract_fusion
  133.1 0.0 collective-permute-done.other
  133.1 2.6 %shard_map.107 = (bf16[1,2,64,2048]{3,2,1,0:T(8,128)(2,1)}, f32[2,32,64]{2,1,0:T(8,128)}) custom-call(s32[4]{0:T(128)} %pad_add_fusion.place, f32[4,64,256]{2,1,0:T(8,128)S(1)} %all-to-all-done.6.got, f32[4,64,256]{2,1,0:T(8,128)S(1)} %collective-permute-done.other, f32[2,64,32]{2,1,0:T(8,128)S(1)} %get-tuple-element.29.basis, ...), custom_call_target="tpu_custom_call" | custom-call | tf_op jit(solution)/shard_map/pallas_call | solution.py:30
  (10 shorter events, 0.1 us)
Async XLA Ops:
  89.2 31.8 %copy-start = (bf16[1,2,64,2048]{3,2,1,0:T(8,128)(2,1)S(1)}, bf16[1,2,64,2048]{3,2,1,0:T(8,128)(2,1)}, u32[]{:S(2)}) copy-start(bf16[1,2,64,2048]{3,2,1,0:T(8,128)(2,1)} %grad.3) | copy-start | bytes 1572868
  89.3 31.8 %copy-start.1 = (bf16[1,2,64,2048]{3,2,1,0:T(8,128)(2,1)S(1)}, bf16[1,2,64,2048]{3,2,1,0:T(8,128)(2,1)}, u32[]{:S(2)}) copy-start(bf16[1,2,64,2048]{3,2,1,0:T(8,128)(2,1)} %moment.3) | copy-start | bytes 1572868
  115.6 16.8 %copy-start.3 = (f32[2,1,4]{2,1,0:T(1,128)S(1)}, f32[2,1,4]{2,1,0:T(1,128)}, u32[]{:S(2)}) copy-start(f32[2,1,4]{2,1,0:T(1,128)} %param.13) | copy-start | bytes 100
  115.6 17.5 %copy-start.2 = (bf16[1,2,64,2048]{3,2,1,0:T(8,128)(2,1)S(1)}, bf16[1,2,64,2048]{3,2,1,0:T(8,128)(2,1)}, u32[]{:S(2)}) copy-start(bf16[1,2,64,2048]{3,2,1,0:T(8,128)(2,1)} %error.3) | copy-start | bytes 1572868
  117.6 8.9 %all-to-all-start.6 = ((f32[4,64,256]{2,1,0:T(8,128)}), f32[4,64,256]{2,1,0:T(8,128)S(1)}, u32[]{:S(2)}, u32[]{:S(2)}) async-start(f32[4,64,256]{2,1,0:T(8,128)} %get-tuple-element.28), calls=%async_computation.6 | async-start | bytes 524288 | tf_op jit(solution)/shard_map/all_to_all | solution.py:206
  126.6 6.6 %collective-permute-start = (f32[4,64,256]{2,1,0:T(8,128)S(1)}, f32[4,64,256]{2,1,0:T(8,128)S(1)}, u32[]{:S(2)}, u32[]{:S(2)}) collective-permute-start(f32[4,64,256]{2,1,0:T(8,128)S(1)} %all-to-all-done.6.got), channel_id=1, source_target_pairs={{0,1},{1,0},{2,3},{3,2},{4,5},{5,4},{6,7},{7,6},{8,9},{9,8},{10,11... | collective-permute-start | bytes 786440 | tf_op jit(solution)/shard_map/ppermute | solution.py:279
